TPU v7x, 256 devices: a whole 4x4x8 slice. The times are simulated.
256 devices in a mesh: leaf: 32 (over x, y, core), rhs: 8 (over z).
Axes of the slice: x: 4, y: 4, z: 8, core: 2. Of those that a mesh axis runs over, the one named last changes fastest.
Arguments:
- charges: bfloat16 [262144, 4096], P(('leaf', 'rhs')), may hold values from -6 to 6
- leaf_coef: bfloat16 [512, 256, 512], P(('leaf', 'rhs')), may hold values from -0.25 to 0.25
- leaf_rows: int32 [512, 256], P(('leaf', 'rhs')), may hold values from 0 to 511, as said below
- local_interp: bfloat16 [480, 256, 512], P('leaf'), may hold values from -0.25 to 0.25
- top_interp: bfloat16 [7936, 512], P('leaf'), may hold values from -0.25 to 0.25
Outputs:
- subtree_skel: bfloat16 [8192, 4096], P('leaf', 'rhs')
- top_skel: bfloat16 [7936, 4096], P('leaf', 'rhs')
Inputs may be any that keep to these rules, and one draw needn't show every extreme that they name: `leaf_rows`: each row holds 256 distinct positions.
All inputs are finite; a program needn't handle non-finite values.
Results may differ from a plain program's by a relative error of at most 0.012.
Values may be sent and summed in bfloat16 or wider, within the bound.
No kernel may reach another device: no remote copies, remote signals or barrier semaphores. Data moves between devices by JAX's collectives and lax.ppermute only.
A program may use at most 64 MiB of HBM per device.

v0:
```python
import functools

import jax
import jax.numpy as jnp
from jax import lax
from jax.experimental import pallas as pl
from jax.experimental.pallas import tpu as pltpu
from jax.sharding import PartitionSpec as P


BF = jnp.bfloat16
F32 = jnp.float32

ORDER = (4, 3, 5, 2, 6, 1, 7, 0)


def mm(a, b):
    return jnp.dot(a, b, preferred_element_type=F32)


def shift(x, distance):
    leaves, n = lax.axis_size("leaf"), lax.axis_size("rhs")
    pairs = []
    for leaf in range(leaves):
        step = -distance if leaf % 2 else distance
        pairs += [(leaf * n + i, leaf * n + (i + step) % n) for i in range(n)]
    return lax.ppermute(x, ("leaf", "rhs"), pairs)


def column(place, rel, width):
    n = len(ORDER)
    block = (place % n + jnp.where(place < n, rel, n - rel)) % n
    return pl.multiple_of(block * width, width)


def swap(x, bits):
    n = lax.axis_size("leaf")
    return lax.ppermute(x, "leaf", [(i, i ^ bits) for i in range(n)])


def vmem(x):
    return pltpu.with_memory_space_constraint(x, pltpu.VMEM)


def hbm(x):
    return pltpu.with_memory_space_constraint(x, pltpu.HBM)


def paced(x, *after):
    return lax.optimization_barrier((x, *after))[0]


def add(a, b):
    return (a.astype(F32) + b.astype(F32)).astype(BF)


def first_kernel(z_ref, l4, l3, l2, l1, coef, rows, charges, t_ref, out_ref, block, sem):
    width = block.shape[1]
    at = column(z_ref[0], ORDER[0], width)
    copy = pltpu.make_async_copy(charges.at[:, pl.ds(at, width)], block, sem)
    copy.start()
    a = mm(l4[0], l3[0]).astype(BF)
    a = mm(a, l2[0]).astype(BF)
    g = mm(a, l1[0]).astype(BF)
    skel = l1.shape[1]
    size = coef.shape[2]
    for j in range(coef.shape[0]):
        gj = g[:, j * skel : (j + 1) * skel]
        where = lax.broadcasted_iota(jnp.int32, (size, skel), 0)
        pick = jnp.where(where == rows[j : j + 1, :], 1.0, 0.0).astype(BF)
        t = mm(gj, coef[j]) + lax.dot_general(
            gj, pick, (((1,), (1,)), ((), ())), preferred_element_type=F32
        )
        t_ref[:, j * size : (j + 1) * size] = t.astype(BF)
    copy.wait()
    out_ref[...] = mm(t_ref[...], block[...]).astype(BF)


def first_part(z, charges, leaf_coef, leaf_rows, local_interp):
    skel = leaf_coef.shape[1]
    rows_here, cols = charges.shape
    width = cols // len(ORDER)
    vm = pl.BlockSpec(memory_space=pltpu.VMEM)
    spec = pltpu.PrefetchScalarGridSpec(
        num_scalar_prefetch=1,
        grid=(1,),
        in_specs=[
            pl.BlockSpec((1, skel, skel), lambda i, z: (14, 0, z[0] % 8 // 4)),
            pl.BlockSpec((1, skel, skel), lambda i, z: (12 + z[0] % 8 // 4, 0, z[0] // 2 % 2)),
            pl.BlockSpec((1, skel, skel), lambda i, z: (8 + z[0] % 8 // 2, 0, z[0] % 2)),
            pl.BlockSpec((1, skel, 2 * skel), lambda i, z: (z[0] % 8, 0, 0)),
            pl.BlockSpec(leaf_coef.shape, lambda i, z: (0, 0, 0)),
            pl.BlockSpec(leaf_rows.shape, lambda i, z: (0, 0)),
            pl.BlockSpec(memory_space=pl.ANY),
        ],
        out_specs=[vm, vm],
        scratch_shapes=[pltpu.VMEM((rows_here, width), BF), pltpu.SemaphoreType.DMA],
    )
    return pl.pallas_call(
        first_kernel,
        grid_spec=spec,
        out_shape=[pltpu.VMEM((skel, rows_here), BF), pltpu.VMEM((skel, width), BF)],
        compiler_params=pltpu.CompilerParams(vmem_limit_bytes=12 << 20),
        name="first_part",
    )(z, *[hbm(local_interp)] * 4, hbm(leaf_coef), hbm(leaf_rows), hbm(charges))


def blocks_kernel(rels, z_ref, t, charges, *outs):
    width = outs[0].shape[1]
    for rel, out in zip(rels, outs):
        at = column(z_ref[0], rel, width)
        out[...] = mm(t[...], charges[:, pl.ds(at, width)]).astype(BF)


def block_parts(z, t, charges, rels):
    width = charges.shape[1] // len(ORDER)
    vm = pl.BlockSpec(memory_space=pltpu.VMEM)
    return pl.pallas_call(
        functools.partial(blocks_kernel, rels),
        in_specs=[pl.BlockSpec(memory_space=pltpu.SMEM), vm, vm],
        out_specs=[vm] * len(rels),
        out_shape=[pltpu.VMEM((t.shape[0], width), BF) for _ in rels],
        compiler_params=pltpu.CompilerParams(vmem_limit_bytes=8 << 20),
        name="blocks",
    )(z, vmem(t), vmem(charges))


def ring_sum(s, m):
    half = s[0].shape[0] // 2
    p = shift(s[4][:half], 1)
    n = shift(s[4][half:], -1)
    m = paced(m, s[4])
    x2 = swap(m[240:248], 16)
    x1 = swap(m[224:248], 8)
    x3 = swap(m[240:248], 24)

    up = jnp.concatenate([add(s[3][:half], p), s[3][half:]], 0)
    down = jnp.concatenate([s[5][:half], add(s[5][half:], n)], 0)
    p = shift(up, 1)
    n = shift(down, -1)
    x1, x2, x3, _, _ = lax.optimization_barrier((x1, x2, x3, up, down))
    v = jnp.concatenate([m[0:240], x1[0:16], m[240:248], x1[16:24], x2, x3], 0)
    y1 = swap(v[128:288], 2)
    up, down = add(s[2], p), add(s[6], n)
    p = shift(up, 1)
    n = shift(down, -1)
    y1 = paced(y1, up, down)
    y2 = swap(jnp.concatenate([v[192:288], y1[64:160]], 0), 4)
    up, down = add(s[1], p), add(s[7], n)
    p = shift(up, 1)
    n = shift(down, -1)
    w = jnp.concatenate([v, y1, paced(y2, up, down)], 0)
    wp = swap(w, 1)
    return (s[0].astype(F32) + p.astype(F32) + n.astype(F32)).astype(BF), w, wp


def compose_kernel(pos, w, wp, q_ref, p1_ref, pn):
    x, y, c = pos[0] // 8, pos[0] // 2 % 4, pos[0] % 2
    both = ((w, c), (wp, 1 - c))
    base = (128, 288, 448 - 64, 544 - 64)

    def half(ref, at, count, h):
        return ref[at : at + count, pl.ds(pl.multiple_of(h * 256, 256), 256)]

    def put(at, size, value):
        pn[pl.ds(pl.multiple_of(at * size, size), size), :] = value

    for ref, core in both:
        at = pl.ds(pl.multiple_of(core * 128, 128), 128)
        p1_ref[at, 0:256] = half(ref, 0, 128, c)
        p1_ref[at, 256:512] = half(ref, 0, 128, 1 - c)
    h2, h3, h4, h5 = y % 2, y // 2, x % 2, x // 2
    for ref, core in both:
        for ky in (0, 1):
            put((y ^ ky) % 2 * 2 + core, 64, half(ref, base[ky], 64, h2))
    q2 = pn[...]
    for ref, core in both:
        for ky in range(4):
            put((y ^ ky) * 2 + core, 32, half(ref, base[ky] + 64, 32, h3))
    q3 = mm(pn[...], q2).astype(BF)
    for ref, core in both:
        for ky in range(4):
            for kx in (0, 1):
                put((x ^ kx) % 2 * 8 + (y ^ ky) * 2 + core, 16, half(ref, base[ky] + 96 + 16 * kx, 16, h4))
    q4 = mm(pn[...], q3).astype(BF)

    r3 = [mm(half(w, base[ky] + 64, 32, h3), q2) for ky in range(4)]
    r4 = [mm(half(w, base[ky] + 96, 32, h4), q3) for ky in range(4)]
    r5 = [mm(half(w, base[ky] + 128, 32, h5), q4) for ky in range(4)]

    def level4(kx):
        return [r4[ky][16 * kx : 16 * kx + 16] for ky in range(4)]

    def level5(kx):
        return [r5[ky][8 * kx : 8 * kx + 8] for ky in range(4)]

    q_ref[0:160, :] = jnp.concatenate(level4(1) + level5(1) + level5(2) + level5(3), 0).astype(BF)
    q_ref[160:224, :] = half(w, base[0], 64, h2)
    q_ref[224:288, :] = half(w, base[1], 64, h2)
    q_ref[288:512, :] = jnp.concatenate(r3 + level4(0) + level5(0), 0).astype(BF)


def compose(pos, w, wp):
    vm = pl.BlockSpec(memory_space=pltpu.VMEM)
    return pl.pallas_call(
        compose_kernel,
        in_specs=[pl.BlockSpec(memory_space=pltpu.SMEM), vm, vm],
        out_specs=[vm, vm],
        out_shape=[pltpu.VMEM((512, 256), BF), pltpu.VMEM((256, 512), BF)],
        scratch_shapes=[pltpu.VMEM((256, 256), BF)],
        compiler_params=pltpu.CompilerParams(vmem_limit_bytes=8 << 20),
        name="compose",
    )(pos, vmem(w), vmem(wp))


def upper(pos, q, p1, root):
    other = swap(root, 1)
    n1 = (mm(p1[:, :256], root) + mm(p1[:, 256:], other)).astype(BF)
    first = lax.dynamic_slice_in_dim(n1, pos % 2 * 128, 128, 0)
    y = mm(q, n1).astype(BF)
    a2 = swap(y[96:128], 16)
    a1 = swap(y[0:96], 8)
    a3 = swap(y[128:160], 24)
    l2, l3 = y[160:288], y[288:416]
    l4 = add(y[416:480], a1[0:64])
    l5 = (
        y[480:512].astype(F32) + a1[64:96].astype(F32) + a2.astype(F32) + a3.astype(F32)
    ).astype(BF)

    def rows(k):
        return [l3[32 * k : 32 * k + 32], l4[16 * k : 16 * k + 16], l5[8 * k : 8 * k + 8]]

    b2 = swap(jnp.concatenate(rows(2), 0), 4)
    b1 = swap(jnp.concatenate([l2[64:128]] + rows(1), 0), 2)
    b3 = swap(jnp.concatenate(rows(3), 0), 6)
    near = add(l2[0:64], b1[0:64])
    far = (
        jnp.concatenate(rows(0), 0).astype(F32)
        + b1[64:120].astype(F32)
        + b2.astype(F32)
        + b3.astype(F32)
    ).astype(BF)
    return jnp.concatenate([first, near, far], 0)


def local(charges, leaf_coef, leaf_rows, local_interp, top_interp):
    pos = lax.axis_index("leaf").astype(jnp.int32)
    z = (pos % 2 * lax.axis_size("rhs") + lax.axis_index("rhs").astype(jnp.int32)).reshape(1)
    s = {}
    t, s[4] = first_part(z, charges, leaf_coef, leaf_rows, local_interp)
    for rels in ((3, 5), (2, 6), (1, 7, 0)):
        for rel, part in zip(rels, block_parts(z, t, charges, rels)):
            s[rel] = part
    root, w, wp = ring_sum(s, top_interp)
    q, p1 = compose(pos.reshape(1), w, wp)
    return root, upper(pos, q, p1, root)


def solution(mesh):
    placed = (
        P(("leaf", "rhs"), None),
        P(("leaf", "rhs"), None, None),
        P(("leaf", "rhs"), None),
        P("leaf", None, None),
        P("leaf", None),
    )

    return jax.shard_map(
        local,
        mesh=mesh,
        in_specs=placed,
        out_specs=(P("leaf", "rhs"), P("leaf", "rhs")),
        check_vma=False,
    )
```

profile of v0, /device:TPU:96, one launch (start us, length us, event | category | flops | bytes accessed | tf_op | source)
XLA Modules:
  0.0 68.4 jit_solution(18032065239744190821)
XLA Ops:
  0.7 3.9 %first_part.1 = (bf16[256,1024]{1,0:T(8,128)(2,1)S(1)}, bf16[256,512]{1,0:T(8,128)(2,1)S(1)}) custom-call(s32[1]{0:T(128)} %bitcast.z_ref, bf16[15,256,512]{2,1,0:T(8,128)(2,1)} %l1.1, bf16[15,256,512]{2,1,0:T(8,128)(2,1)} %l1.1, bf16[15,256,512]{2,1,0:T(8,128)(2,1)} %l1.1, bf16[15,256,512]{2,1,0:T(8,128)(2,1)} %l1.1, bf16[2,256,512]{2,1,0:T(8,128)(2,1)} %coef.1, ...), custom_call_target="tpu_custom_call" | custom-call | tf_op jit(solution)/shard_map/first_part/pallas_call | solution.py:99
  4.6 2.8 %collective-permute-start.10 = (bf16[8,512]{1,0:T(8,128)(2,1)S(1)}, bf16[8,512]{1,0:T(8,128)(2,1)S(1)}, u32[]{:S(2)}, u32[]{:S(2)}) collective-permute-start(bf16[8,512]{1,0:T(8,128)(2,1)S(1)} %slice.135), channel_id=1, source_target_pairs={{0,192},{8,200},{16,208},{24,216},{32,224},{40,232},{48,240},{56,2... | collective-permute-start | bytes 24584 | tf_op jit(solution)/shard_map/ppermute | solution.py:38
  7.4 0.8 %collective-permute-start.9 = (bf16[8,512]{1,0:T(8,128)(2,1)S(1)}, bf16[8,512]{1,0:T(8,128)(2,1)S(1)}, u32[]{:S(2)}, u32[]{:S(2)}) collective-permute-start(bf16[8,512]{1,0:T(8,128)(2,1)S(1)} %slice.135), channel_id=1, source_target_pairs={{0,128},{8,136},{16,144},{24,152},{32,160},{40,168},{48,176},{56,1... | collective-permute-start | bytes 24584 | tf_op jit(solution)/shard_map/ppermute | solution.py:38
  8.3 3.2 %collective-permute-start = (bf16[128,512]{1,0:T(8,128)(2,1)S(1)}, bf16[128,512]{1,0:T(8,128)(2,1)S(1)}, u32[]{:S(2)}, u32[]{:S(2)}) collective-permute-start(bf16[128,512]{1,0:T(8,128)(2,1)S(1)} %get-tuple-element.42), channel_id=1, source_target_pairs={{0,1},{1,2},{2,3},{3,4},{4,5},{5,6},{6,7},{7,0},{8,15},{9,8},{10,9... | collective-permute-start | bytes 393224 | tf_op jit(solution)/shard_map/ppermute | solution.py:27
  12.7 0.7 %blocks.4 = (bf16[256,512]{1,0:T(8,128)(2,1)S(1)}, bf16[256,512]{1,0:T(8,128)(2,1)S(1)}) custom-call(s32[1]{0:T(128)} %bitcast.z_ref, bf16[256,1024]{1,0:T(8,128)(2,1)S(1)} %get-tuple-element.19.t, bf16[1024,4096]{1,0:T(8,128)(2,1)S(1)} %copy-done), custom_call_target="tpu_custom_call" | custom-call | tf_op jit(solution)/shard_map/blocks/pallas_call | solution.py:118
  13.5 1.0 %blocks.3 = (bf16[256,512]{1,0:T(8,128)(2,1)S(1)}, bf16[256,512]{1,0:T(8,128)(2,1)S(1)}, bf16[256,512]{1,0:T(8,128)(2,1)S(1)}) custom-call(s32[1]{0:T(128)} %bitcast.z_ref, bf16[256,1024]{1,0:T(8,128)(2,1)S(1)} %get-tuple-element.19.t, bf16[1024,4096]{1,0:T(8,128)(2,1)S(1)} %copy-done), custom_call_target="tpu_custom_call" | custom-call | tf_op jit(solution)/shard_map/blocks/pallas_call | solution.py:118
  14.6 3.3 %collective-permute-start.1 = (bf16[256,512]{1,0:T(8,128)(2,1)S(1)}, bf16[256,512]{1,0:T(8,128)(2,1)S(1)}, u32[]{:S(2)}, u32[]{:S(2)}) collective-permute-start(bf16[256,512]{1,0:T(8,128)(2,1)S(1)} %pad_maximum_fusion), channel_id=1, source_target_pairs={{0,1},{1,2},{2,3},{3,4},{4,5},{5,6},{6,7},{7,0},{8,15},{9,8},{10,9... | collective-permute-start | bytes 786440 | tf_op jit(solution)/shard_map/ppermute | solution.py:27
  18.3 1.7 %collective-permute-start.11 = (bf16[160,512]{1,0:T(8,128)(2,1)S(1)}, bf16[160,512]{1,0:T(8,128)(2,1)S(1)}, u32[]{:S(2)}, u32[]{:S(2)}) collective-permute-start(bf16[160,512]{1,0:T(8,128)(2,1)S(1)} %slice.166), channel_id=1, source_target_pairs={{0,16},{8,24},{16,0},{24,8},{32,48},{40,56},{48,32},{56,40},{64,80... | collective-permute-start | bytes 491528 | tf_op jit(solution)/shard_map/ppermute | solution.py:38
  19.9 2.4 %collective-permute-done.1 = bf16[256,512]{1,0:T(8,128)(2,1)S(1)} collective-permute-done((bf16[256,512]{1,0:T(8,128)(2,1)S(1)}, bf16[256,512]{1,0:T(8,128)(2,1)S(1)}, u32[]{:S(2)}, u32[]{:S(2)}) %collective-permute-start.1) | collective-permute-done | bytes 262176 | tf_op jit(solution)/shard_map/ppermute | solution.py:27
  22.4 3.8 %collective-permute-start.2 = (bf16[256,512]{1,0:T(8,128)(2,1)S(1)}, bf16[256,512]{1,0:T(8,128)(2,1)S(1)}, u32[]{:S(2)}, u32[]{:S(2)}) collective-permute-start(bf16[256,512]{1,0:T(8,128)(2,1)S(1)} %add_convert_fusion.4), channel_id=1, source_target_pairs={{0,1},{1,2},{2,3},{3,4},{4,5},{5,6},{6,7},{7,0},{8,15},{9,8},{10,9... | collective-permute-start | bytes 786440 | tf_op jit(solution)/shard_map/ppermute | solution.py:27
  26.2 1.0 %collective-permute-done.5 = bf16[256,512]{1,0:T(8,128)(2,1)S(1)} collective-permute-done((bf16[256,512]{1,0:T(8,128)(2,1)S(1)}, bf16[256,512]{1,0:T(8,128)(2,1)S(1)}, u32[]{:S(2)}, u32[]{:S(2)}) %collective-permute-start.5) | collective-permute-done | bytes 262176 | tf_op jit(solution)/shard_map/ppermute | solution.py:27
  27.4 3.3 %collective-permute-start.12 = (bf16[192,512]{1,0:T(8,128)(2,1)S(1)}, bf16[192,512]{1,0:T(8,128)(2,1)S(1)}, u32[]{:S(2)}, u32[]{:S(2)}) collective-permute-start(bf16[192,512]{1,0:T(8,128)(2,1)S(1)} %pad_maximum_fusion.3), channel_id=1, source_target_pairs={{0,32},{8,40},{16,48},{24,56},{32,0},{40,8},{48,16},{56,24},{64,96... | collective-permute-start | bytes 589832 | tf_op jit(solution)/shard_map/ppermute | solution.py:38
  30.7 3.3 %collective-permute-start.3 = (bf16[256,512]{1,0:T(8,128)(2,1)S(1)}, bf16[256,512]{1,0:T(8,128)(2,1)S(1)}, u32[]{:S(2)}, u32[]{:S(2)}) collective-permute-start(bf16[256,512]{1,0:T(8,128)(2,1)S(1)} %add_convert_fusion.3), channel_id=1, source_target_pairs={{0,1},{1,2},{2,3},{3,4},{4,5},{5,6},{6,7},{7,0},{8,15},{9,8},{10,9... | collective-permute-start | bytes 786440 | tf_op jit(solution)/shard_map/ppermute | solution.py:27
  34.0 3.5 %collective-permute-done.6 = bf16[256,512]{1,0:T(8,128)(2,1)S(1)} collective-permute-done((bf16[256,512]{1,0:T(8,128)(2,1)S(1)}, bf16[256,512]{1,0:T(8,128)(2,1)S(1)}, u32[]{:S(2)}, u32[]{:S(2)}) %collective-permute-start.6) | collective-permute-done | bytes 262176 | tf_op jit(solution)/shard_map/ppermute | solution.py:27
  38.1 7.2 %collective-permute-done.7 = bf16[256,512]{1,0:T(8,128)(2,1)S(1)} collective-permute-done((bf16[256,512]{1,0:T(8,128)(2,1)S(1)}, bf16[256,512]{1,0:T(8,128)(2,1)S(1)}, u32[]{:S(2)}, u32[]{:S(2)}) %collective-permute-start.7) | collective-permute-done | bytes 262176 | tf_op jit(solution)/shard_map/ppermute | solution.py:27
  46.1 0.9 %collective-permute-done.14 = bf16[256,512]{1,0:T(8,128)(2,1)S(1)} collective-permute-done((bf16[256,512]{1,0:T(8,128)(2,1)S(1)}, bf16[256,512]{1,0:T(8,128)(2,1)S(1)}, u32[]{:S(2)}, u32[]{:S(2)}) %collective-permute-start.14) | collective-permute-done | bytes 262176 | tf_op jit(solution)/shard_map/ppermute | solution.py:38
  47.8 1.9 %collective-permute-start.15 = (bf16[96,512]{1,0:T(8,128)(2,1)S(1)}, bf16[96,512]{1,0:T(8,128)(2,1)S(1)}, u32[]{:S(2)}, u32[]{:S(2)}) collective-permute-start(bf16[96,512]{1,0:T(8,128)(2,1)S(1)} %slice.172), channel_id=1, source_target_pairs={{0,64},{8,72},{16,80},{24,88},{32,96},{40,104},{48,112},{56,120},{... | collective-permute-start | bytes 294920 | tf_op jit(solution)/shard_map/ppermute | solution.py:38
  49.7 2.7 %collective-permute-start.16 = (bf16[32,512]{1,0:T(8,128)(2,1)S(1)}, bf16[32,512]{1,0:T(8,128)(2,1)S(1)}, u32[]{:S(2)}, u32[]{:S(2)}) collective-permute-start(bf16[32,512]{1,0:T(8,128)(2,1)S(1)} %get-tuple-element.40), channel_id=1, source_target_pairs={{0,128},{8,136},{16,144},{24,152},{32,160},{40,168},{48,176},{56,1... | collective-permute-start | bytes 98312 | tf_op jit(solution)/shard_map/ppermute | solution.py:38
  52.9 3.1 %collective-permute-done.16 = bf16[32,512]{1,0:T(8,128)(2,1)S(1)} collective-permute-done((bf16[32,512]{1,0:T(8,128)(2,1)S(1)}, bf16[32,512]{1,0:T(8,128)(2,1)S(1)}, u32[]{:S(2)}, u32[]{:S(2)}) %collective-permute-start.16) | collective-permute-done | bytes 32800 | tf_op jit(solution)/shard_map/ppermute | solution.py:38
  56.0 1.6 %collective-permute-done.17 = bf16[32,512]{1,0:T(8,128)(2,1)S(1)} collective-permute-done((bf16[32,512]{1,0:T(8,128)(2,1)S(1)}, bf16[32,512]{1,0:T(8,128)(2,1)S(1)}, u32[]{:S(2)}, u32[]{:S(2)}) %collective-permute-start.17) | collective-permute-done | bytes 32800 | tf_op jit(solution)/shard_map/ppermute | solution.py:38
  57.6 1.7 %collective-permute-start.18 = (bf16[120,512]{1,0:T(8,128)(2,1)S(1)}, bf16[120,512]{1,0:T(8,128)(2,1)S(1)}, u32[]{:S(2)}, u32[]{:S(2)}) collective-permute-start(bf16[120,512]{1,0:T(8,128)(2,1)S(1)} %pad_maximum_fusion.4), channel_id=1, source_target_pairs={{0,16},{8,24},{16,0},{24,8},{32,48},{40,56},{48,32},{56,40},{64,80... | collective-permute-start | bytes 368648 | tf_op jit(solution)/shard_map/ppermute | solution.py:38
  59.3 2.9 %collective-permute-start.19 = (bf16[56,512]{1,0:T(8,128)(2,1)S(1)}, bf16[56,512]{1,0:T(8,128)(2,1)S(1)}, u32[]{:S(2)}, u32[]{:S(2)}) collective-permute-start(bf16[56,512]{1,0:T(8,128)(2,1)S(1)} %pad_maximum_fusion.5), channel_id=1, source_target_pairs={{0,32},{8,40},{16,48},{24,56},{32,0},{40,8},{48,16},{56,24},{64,96... | collective-permute-start | bytes 172040 | tf_op jit(solution)/shard_map/ppermute | solution.py:38
  63.2 2.5 %collective-permute-done.19 = bf16[56,512]{1,0:T(8,128)(2,1)S(1)} collective-permute-done((bf16[56,512]{1,0:T(8,128)(2,1)S(1)}, bf16[56,512]{1,0:T(8,128)(2,1)S(1)}, u32[]{:S(2)}, u32[]{:S(2)}) %collective-permute-start.19) | collective-permute-done | bytes 57376 | tf_op jit(solution)/shard_map/ppermute | solution.py:38
  65.7 1.9 %collective-permute-done.20 = bf16[56,512]{1,0:T(8,128)(2,1)S(1)} collective-permute-done((bf16[56,512]{1,0:T(8,128)(2,1)S(1)}, bf16[56,512]{1,0:T(8,128)(2,1)S(1)}, u32[]{:S(2)}, u32[]{:S(2)}) %collective-permute-start.20) | collective-permute-done | bytes 57376 | tf_op jit(solution)/shard_map/ppermute | solution.py:38
  (72 shorter events, 6.1 us)
Async XLA Ops:
  0.6 3.9 %copy-start.2 = (bf16[248,512]{1,0:T(8,128)(2,1)S(1)}, bf16[248,512]{1,0:T(8,128)(2,1)}, u32[]{:S(2)}) copy-start(bf16[248,512]{1,0:T(8,128)(2,1)} %param.9) | copy-start | bytes 761860
  0.7 11.4 %copy-start = (bf16[1024,4096]{1,0:T(8,128)(2,1)S(1)}, bf16[1024,4096]{1,0:T(8,128)(2,1)}, u32[]{:S(2)}) copy-start(bf16[1024,4096]{1,0:T(8,128)(2,1)} %charges.7) | copy-start | bytes 25165828
  4.6 13.5 %collective-permute-start.10 = (bf16[8,512]{1,0:T(8,128)(2,1)S(1)}, bf16[8,512]{1,0:T(8,128)(2,1)S(1)}, u32[]{:S(2)}, u32[]{:S(2)}) collective-permute-start(bf16[8,512]{1,0:T(8,128)(2,1)S(1)} %slice.135), channel_id=1, source_target_pairs={{0,192},{8,200},{16,208},{24,216},{32,224},{40,232},{48,240},{56,2... | collective-permute-start | bytes 24584 | tf_op jit(solution)/shard_map/ppermute | solution.py:38
  7.4 10.7 %collective-permute-start.9 = (bf16[8,512]{1,0:T(8,128)(2,1)S(1)}, bf16[8,512]{1,0:T(8,128)(2,1)S(1)}, u32[]{:S(2)}, u32[]{:S(2)}) collective-permute-start(bf16[8,512]{1,0:T(8,128)(2,1)S(1)} %slice.135), channel_id=1, source_target_pairs={{0,128},{8,136},{16,144},{24,152},{32,160},{40,168},{48,176},{56,1... | collective-permute-start | bytes 24584 | tf_op jit(solution)/shard_map/ppermute | solution.py:38
  8.3 6.3 %collective-permute-start = (bf16[128,512]{1,0:T(8,128)(2,1)S(1)}, bf16[128,512]{1,0:T(8,128)(2,1)S(1)}, u32[]{:S(2)}, u32[]{:S(2)}) collective-permute-start(bf16[128,512]{1,0:T(8,128)(2,1)S(1)} %get-tuple-element.42), channel_id=1, source_target_pairs={{0,1},{1,2},{2,3},{3,4},{4,5},{5,6},{6,7},{7,0},{8,15},{9,8},{10,9... | collective-permute-start | bytes 393224 | tf_op jit(solution)/shard_map/ppermute | solution.py:27
  11.5 6.5 %collective-permute-start.4 = (bf16[128,512]{1,0:T(8,128)(2,1)S(1)}, bf16[128,512]{1,0:T(8,128)(2,1)S(1)}, u32[]{:S(2)}, u32[]{:S(2)}) collective-permute-start(bf16[128,512]{1,0:T(8,128)(2,1)S(1)} %get-tuple-element.43), channel_id=1, source_target_pairs={{0,7},{1,0},{2,1},{3,2},{4,3},{5,4},{6,5},{7,6},{8,9},{9,10},{10,1... | collective-permute-start | bytes 393224 | tf_op jit(solution)/shard_map/ppermute | solution.py:27
  11.5 6.7 %collective-permute-start.8 = (bf16[24,512]{1,0:T(8,128)(2,1)S(1)}, bf16[24,512]{1,0:T(8,128)(2,1)S(1)}, u32[]{:S(2)}, u32[]{:S(2)}) collective-permute-start(bf16[24,512]{1,0:T(8,128)(2,1)S(1)} %slice.134), channel_id=1, source_target_pairs={{0,64},{8,72},{16,80},{24,88},{32,96},{40,104},{48,112},{56,120},{... | collective-permute-start | bytes 73736 | tf_op jit(solution)/shard_map/ppermute | solution.py:38
  14.6 7.7 %collective-permute-start.1 = (bf16[256,512]{1,0:T(8,128)(2,1)S(1)}, bf16[256,512]{1,0:T(8,128)(2,1)S(1)}, u32[]{:S(2)}, u32[]{:S(2)}) collective-permute-start(bf16[256,512]{1,0:T(8,128)(2,1)S(1)} %pad_maximum_fusion), channel_id=1, source_target_pairs={{0,1},{1,2},{2,3},{3,4},{4,5},{5,6},{6,7},{7,0},{8,15},{9,8},{10,9... | collective-permute-start | bytes 786440 | tf_op jit(solution)/shard_map/ppermute | solution.py:27
  18.1 9.1 %collective-permute-start.5 = (bf16[256,512]{1,0:T(8,128)(2,1)S(1)}, bf16[256,512]{1,0:T(8,128)(2,1)S(1)}, u32[]{:S(2)}, u32[]{:S(2)}) collective-permute-start(bf16[256,512]{1,0:T(8,128)(2,1)S(1)} %pad_maximum_fusion.1), channel_id=1, source_target_pairs={{0,7},{1,0},{2,1},{3,2},{4,3},{5,4},{6,5},{7,6},{8,9},{9,10},{10,1... | collective-permute-start | bytes 786440 | tf_op jit(solution)/shard_map/ppermute | solution.py:27
  18.3 9.1 %collective-permute-start.11 = (bf16[160,512]{1,0:T(8,128)(2,1)S(1)}, bf16[160,512]{1,0:T(8,128)(2,1)S(1)}, u32[]{:S(2)}, u32[]{:S(2)}) collective-permute-start(bf16[160,512]{1,0:T(8,128)(2,1)S(1)} %slice.166), channel_id=1, source_target_pairs={{0,16},{8,24},{16,0},{24,8},{32,48},{40,56},{48,32},{56,40},{64,80... | collective-permute-start | bytes 491528 | tf_op jit(solution)/shard_map/ppermute | solution.py:38
  22.4 8.3 %collective-permute-start.2 = (bf16[256,512]{1,0:T(8,128)(2,1)S(1)}, bf16[256,512]{1,0:T(8,128)(2,1)S(1)}, u32[]{:S(2)}, u32[]{:S(2)}) collective-permute-start(bf16[256,512]{1,0:T(8,128)(2,1)S(1)} %add_convert_fusion.4), channel_id=1, source_target_pairs={{0,1},{1,2},{2,3},{3,4},{4,5},{5,6},{6,7},{7,0},{8,15},{9,8},{10,9... | collective-permute-start | bytes 786440 | tf_op jit(solution)/shard_map/ppermute | solution.py:27
  27.3 10.3 %collective-permute-start.6 = (bf16[256,512]{1,0:T(8,128)(2,1)S(1)}, bf16[256,512]{1,0:T(8,128)(2,1)S(1)}, u32[]{:S(2)}, u32[]{:S(2)}) collective-permute-start(bf16[256,512]{1,0:T(8,128)(2,1)S(1)} %add_convert_fusion.2), channel_id=1, source_target_pairs={{0,7},{1,0},{2,1},{3,2},{4,3},{5,4},{6,5},{7,6},{8,9},{9,10},{10,1... | collective-permute-start | bytes 786440 | tf_op jit(solution)/shard_map/ppermute | solution.py:27
  27.4 10.3 %collective-permute-start.12 = (bf16[192,512]{1,0:T(8,128)(2,1)S(1)}, bf16[192,512]{1,0:T(8,128)(2,1)S(1)}, u32[]{:S(2)}, u32[]{:S(2)}) collective-permute-start(bf16[192,512]{1,0:T(8,128)(2,1)S(1)} %pad_maximum_fusion.3), channel_id=1, source_target_pairs={{0,32},{8,40},{16,48},{24,56},{32,0},{40,8},{48,16},{56,24},{64,96... | collective-permute-start | bytes 589832 | tf_op jit(solution)/shard_map/ppermute | solution.py:38
  30.7 7.3 %collective-permute-start.3 = (bf16[256,512]{1,0:T(8,128)(2,1)S(1)}, bf16[256,512]{1,0:T(8,128)(2,1)S(1)}, u32[]{:S(2)}, u32[]{:S(2)}) collective-permute-start(bf16[256,512]{1,0:T(8,128)(2,1)S(1)} %add_convert_fusion.3), channel_id=1, source_target_pairs={{0,1},{1,2},{2,3},{3,4},{4,5},{5,6},{6,7},{7,0},{8,15},{9,8},{10,9... | collective-permute-start | bytes 786440 | tf_op jit(solution)/shard_map/ppermute | solution.py:27
  37.6 7.7 %collective-permute-start.7 = (bf16[256,512]{1,0:T(8,128)(2,1)S(1)}, bf16[256,512]{1,0:T(8,128)(2,1)S(1)}, u32[]{:S(2)}, u32[]{:S(2)}) collective-permute-start(bf16[256,512]{1,0:T(8,128)(2,1)S(1)} %add_convert_fusion.1), channel_id=1, source_target_pairs={{0,7},{1,0},{2,1},{3,2},{4,3},{5,4},{6,5},{7,6},{8,9},{9,10},{10,1... | collective-permute-start | bytes 786440 | tf_op jit(solution)/shard_map/ppermute | solution.py:27
  37.8 7.7 %collective-permute-start.13 = (bf16[640,512]{1,0:T(8,128)(2,1)S(1)}, bf16[640,512]{1,0:T(8,128)(2,1)S(1)}, u32[]{:S(2)}, u32[]{:S(2)}) collective-permute-start(bf16[640,512]{1,0:T(8,128)(2,1)S(1)} %constant_dynamic-update-slice_fusion.5.w), channel_id=1, source_target_pairs={{0,8},{8,0},{16,24},{24,16},{32,40},{40,32},{48,56},{56,48},{64,72... | collective-permute-start | bytes 1966088 | tf_op jit(solution)/shard_map/ppermute | solution.py:38
  45.4 23.0 %copy-start.1 = (bf16[256,512]{1,0:T(8,128)(2,1)}, bf16[256,512]{1,0:T(8,128)(2,1)S(1)}, u32[]{:S(2)}) copy-start(bf16[256,512]{1,0:T(8,128)(2,1)S(1)} %add_convert_fusion) | copy-start | bytes 786436
  45.4 1.6 %collective-permute-start.14 = (bf16[256,512]{1,0:T(8,128)(2,1)S(1)}, bf16[256,512]{1,0:T(8,128)(2,1)S(1)}, u32[]{:S(2)}, u32[]{:S(2)}) collective-permute-start(bf16[256,512]{1,0:T(8,128)(2,1)S(1)} %add_convert_fusion), channel_id=1, source_target_pairs={{0,8},{8,0},{16,24},{24,16},{32,40},{40,32},{48,56},{56,48},{64,72... | collective-permute-start | bytes 786440 | tf_op jit(solution)/shard_map/ppermute | solution.py:38
  47.8 5.0 %collective-permute-start.15 = (bf16[96,512]{1,0:T(8,128)(2,1)S(1)}, bf16[96,512]{1,0:T(8,128)(2,1)S(1)}, u32[]{:S(2)}, u32[]{:S(2)}) collective-permute-start(bf16[96,512]{1,0:T(8,128)(2,1)S(1)} %slice.172), channel_id=1, source_target_pairs={{0,64},{8,72},{16,80},{24,88},{32,96},{40,104},{48,112},{56,120},{... | collective-permute-start | bytes 294920 | tf_op jit(solution)/shard_map/ppermute | solution.py:38
  49.7 6.3 %collective-permute-start.16 = (bf16[32,512]{1,0:T(8,128)(2,1)S(1)}, bf16[32,512]{1,0:T(8,128)(2,1)S(1)}, u32[]{:S(2)}, u32[]{:S(2)}) collective-permute-start(bf16[32,512]{1,0:T(8,128)(2,1)S(1)} %get-tuple-element.40), channel_id=1, source_target_pairs={{0,128},{8,136},{16,144},{24,152},{32,160},{40,168},{48,176},{56,1... | collective-permute-start | bytes 98312 | tf_op jit(solution)/shard_map/ppermute | solution.py:38
  52.5 5.1 %collective-permute-start.17 = (bf16[32,512]{1,0:T(8,128)(2,1)S(1)}, bf16[32,512]{1,0:T(8,128)(2,1)S(1)}, u32[]{:S(2)}, u32[]{:S(2)}) collective-permute-start(bf16[32,512]{1,0:T(8,128)(2,1)S(1)} %get-tuple-element.39), channel_id=1, source_target_pairs={{0,192},{8,200},{16,208},{24,216},{32,224},{40,232},{48,240},{56,2... | collective-permute-start | bytes 98312 | tf_op jit(solution)/shard_map/ppermute | solution.py:38
  57.6 5.5 %collective-permute-start.18 = (bf16[120,512]{1,0:T(8,128)(2,1)S(1)}, bf16[120,512]{1,0:T(8,128)(2,1)S(1)}, u32[]{:S(2)}, u32[]{:S(2)}) collective-permute-start(bf16[120,512]{1,0:T(8,128)(2,1)S(1)} %pad_maximum_fusion.4), channel_id=1, source_target_pairs={{0,16},{8,24},{16,0},{24,8},{32,48},{40,56},{48,32},{56,40},{64,80... | collective-permute-start | bytes 368648 | tf_op jit(solution)/shard_map/ppermute | solution.py:38
  59.3 6.4 %collective-permute-start.19 = (bf16[56,512]{1,0:T(8,128)(2,1)S(1)}, bf16[56,512]{1,0:T(8,128)(2,1)S(1)}, u32[]{:S(2)}, u32[]{:S(2)}) collective-permute-start(bf16[56,512]{1,0:T(8,128)(2,1)S(1)} %pad_maximum_fusion.5), channel_id=1, source_target_pairs={{0,32},{8,40},{16,48},{24,56},{32,0},{40,8},{48,16},{56,24},{64,96... | collective-permute-start | bytes 172040 | tf_op jit(solution)/shard_map/ppermute | solution.py:38
  62.2 5.4 %collective-permute-start.20 = (bf16[56,512]{1,0:T(8,128)(2,1)S(1)}, bf16[56,512]{1,0:T(8,128)(2,1)S(1)}, u32[]{:S(2)}, u32[]{:S(2)}) collective-permute-start(bf16[56,512]{1,0:T(8,128)(2,1)S(1)} %pad_maximum_fusion.6), channel_id=1, source_target_pairs={{0,48},{8,56},{16,32},{24,40},{32,16},{40,24},{48,0},{56,8},{64,11... | collective-permute-start | bytes 172040 | tf_op jit(solution)/shard_map/ppermute | solution.py:38
where the time goes:
time: 68.5 us; the launch traced here: 68.4 us
  starting transfers between devices  32.9 us (48%)
  waiting for transfers between devices  25.2 us (37%)
  Pallas kernels  6.97 us (10%)
  other arithmetic  1.32 us (2%)
  between operations  1.09 us (2%)
  matrix products  0.74 us (1%)
    ppermute x13, starting transfers between devices, swap(): return lax.ppermute(x, 'leaf', [(i, i ^ bits) for i in range(n)])  19 us
    ppermute x8, waiting for transfers between devices, shift(): return lax.ppermute(x, ('leaf', 'rhs'), pairs)  14.2 us
    ppermute x8, starting transfers between devices, shift(): return lax.ppermute(x, ('leaf', 'rhs'), pairs)  13.8 us
    ppermute x13, waiting for transfers between devices, swap(): return lax.ppermute(x, 'leaf', [(i, i ^ bits) for i in range(n)])  11 us
    pallas_call x1, Pallas kernels, first_part(): pl.pallas_call(first_kernel, grid_spec=spec, out_shape=[pltpu.VMEM((skel,...  3.9 us
    pallas_call x3, Pallas kernels, block_parts(): pl.pallas_call(functools.partial(blocks_kernel, rels), in_specs=[pl.Block...  2.43 us
  transfers between devices with their start and end apart: 21, of which 11 were waited for; matrix products, arithmetic and copies ran while one was open for 1% of the time, Pallas kernels for 4%

commit v1 on v0

--- a/solution.py
+++ b/solution.py
@@ -22,14 +22,14 @@
     leaves, n = lax.axis_size("leaf"), lax.axis_size("rhs")
     pairs = []
     for leaf in range(leaves):
-        step = -distance if leaf % 2 else distance
+        step = distance
         pairs += [(leaf * n + i, leaf * n + (i + step) % n) for i in range(n)]
     return lax.ppermute(x, ("leaf", "rhs"), pairs)
 
 
 def column(place, rel, width):
     n = len(ORDER)
-    block = (place % n + jnp.where(place < n, rel, n - rel)) % n
+    block = (place % n + rel) % n
     return pl.multiple_of(block * width, width)
 
 
@@ -52,6 +52,10 @@
 
 def add(a, b):
     return (a.astype(F32) + b.astype(F32)).astype(BF)
+
+
+def add3(a, b, c):
+    return (a.astype(F32) + b.astype(F32) + c.astype(F32)).astype(BF)
 
 
 def first_kernel(z_ref, l4, l3, l2, l1, coef, rows, charges, t_ref, out_ref, block, sem):
@@ -130,28 +134,29 @@
     p = shift(s[4][:half], 1)
     n = shift(s[4][half:], -1)
     m = paced(m, s[4])
+    x1 = swap(m[224:248], 8)
     x2 = swap(m[240:248], 16)
-    x1 = swap(m[224:248], 8)
     x3 = swap(m[240:248], 24)
 
     up = jnp.concatenate([add(s[3][:half], p), s[3][half:]], 0)
     down = jnp.concatenate([s[5][:half], add(s[5][half:], n)], 0)
     p = shift(up, 1)
     n = shift(down, -1)
-    x1, x2, x3, _, _ = lax.optimization_barrier((x1, x2, x3, up, down))
-    v = jnp.concatenate([m[0:240], x1[0:16], m[240:248], x1[16:24], x2, x3], 0)
-    y1 = swap(v[128:288], 2)
     up, down = add(s[2], p), add(s[6], n)
     p = shift(up, 1)
     n = shift(down, -1)
-    y1 = paced(y1, up, down)
-    y2 = swap(jnp.concatenate([v[192:288], y1[64:160]], 0), 4)
+    x1, x2, x3, _, _ = lax.optimization_barrier((x1, x2, x3, up, down))
+    v = jnp.concatenate([m[0:240], x1[0:16], m[240:248], x1[16:24], x2, x3], 0)
+    y2 = swap(v[192:288], 4)
+    y1 = swap(v[128:288], 2)
+    y3 = swap(v[192:288], 6)
     up, down = add(s[1], p), add(s[7], n)
     p = shift(up, 1)
     n = shift(down, -1)
-    w = jnp.concatenate([v, y1, paced(y2, up, down)], 0)
+    y1, y2, y3, _, _ = lax.optimization_barrier((y1, y2, y3, up, down))
+    w = jnp.concatenate([v, y1, y2, y3], 0)
     wp = swap(w, 1)
-    return (s[0].astype(F32) + p.astype(F32) + n.astype(F32)).astype(BF), w, wp
+    return add3(s[0], p, n), w, wp
 
 
 def compose_kernel(pos, w, wp, q_ref, p1_ref, pn):
@@ -215,7 +220,8 @@
 
 def upper(pos, q, p1, root):
     other = swap(root, 1)
-    n1 = (mm(p1[:, :256], root) + mm(p1[:, 256:], other)).astype(BF)
+    mine = lax.optimization_barrier(mm(p1[:, :256], root))
+    n1 = (mine + mm(p1[:, 256:], other)).astype(BF)
     first = lax.dynamic_slice_in_dim(n1, pos % 2 * 128, 128, 0)
     y = mm(q, n1).astype(BF)
     a2 = swap(y[96:128], 16)

time: 68.5 us -> 70.6 us (1.031)
  the two profiles are of different devices: /device:TPU:96 before, /device:TPU:6 now
where the time goes in v1:
time: 70.6 us; the launch traced here: 69.6 us
  starting transfers between devices  33 us (47%)
  waiting for transfers between devices  26.2 us (37%)
  Pallas kernels  6.97 us (10%)
  other arithmetic  1.4 us (2%)
  between operations  1.07 us (2%)
  matrix products  0.73 us (1%)
    ppermute x8, starting transfers between devices, shift(): return lax.ppermute(x, ('leaf', 'rhs'), pairs)  16.6 us
    ppermute x14, starting transfers between devices, swap(): return lax.ppermute(x, 'leaf', [(i, i ^ bits) for i in range(n)])  16.4 us
    ppermute x8, waiting for transfers between devices, shift(): return lax.ppermute(x, ('leaf', 'rhs'), pairs)  16.4 us
    ppermute x14, waiting for transfers between devices, swap(): return lax.ppermute(x, 'leaf', [(i, i ^ bits) for i in range(n)])  9.86 us
    pallas_call x1, Pallas kernels, first_part(): pl.pallas_call(first_kernel, grid_spec=spec, out_shape=[pltpu.VMEM((skel,...  3.9 us
    pallas_call x3, Pallas kernels, block_parts(): pl.pallas_call(functools.partial(blocks_kernel, rels), in_specs=[pl.Block...  2.45 us
  transfers between devices with their start and end apart: 22, of which 15 were waited for; matrix products, arithmetic and copies ran while one was open for 1% of the time, Pallas kernels for 4%

profile of v1, /device:TPU:6, one launch (start us, length us, event | category | flops | bytes accessed | tf_op | source)
XLA Modules:
  0.0 69.6 jit_solution(1424028452676468007)
XLA Ops:
  0.7 3.9 %first_part.1 = (bf16[256,1024]{1,0:T(8,128)(2,1)S(1)}, bf16[256,512]{1,0:T(8,128)(2,1)S(1)}) custom-call(s32[1]{0:T(128)} %bitcast.z_ref, bf16[15,256,512]{2,1,0:T(8,128)(2,1)} %l1.1, bf16[15,256,512]{2,1,0:T(8,128)(2,1)} %l1.1, bf16[15,256,512]{2,1,0:T(8,128)(2,1)} %l1.1, bf16[15,256,512]{2,1,0:T(8,128)(2,1)} %l1.1, bf16[2,256,512]{2,1,0:T(8,128)(2,1)} %coef.1, ...), custom_call_target="tpu_custom_call" | custom-call | tf_op jit(solution)/shard_map/first_part/pallas_call | solution.py:103
  4.6 5.9 %collective-permute-start.4 = (bf16[128,512]{1,0:T(8,128)(2,1)S(1)}, bf16[128,512]{1,0:T(8,128)(2,1)S(1)}, u32[]{:S(2)}, u32[]{:S(2)}) collective-permute-start(bf16[128,512]{1,0:T(8,128)(2,1)S(1)} %get-tuple-element.45), channel_id=1, source_target_pairs={{0,7},{1,0},{2,1},{3,2},{4,3},{5,4},{6,5},{7,6},{8,15},{9,8},{10,9... | collective-permute-start | bytes 393224 | tf_op jit(solution)/shard_map/ppermute | solution.py:27
  10.5 1.4 %collective-permute-start.9 = (bf16[8,512]{1,0:T(8,128)(2,1)S(1)}, bf16[8,512]{1,0:T(8,128)(2,1)S(1)}, u32[]{:S(2)}, u32[]{:S(2)}) collective-permute-start(bf16[8,512]{1,0:T(8,128)(2,1)S(1)} %slice.133), channel_id=1, source_target_pairs={{0,128},{8,136},{16,144},{24,152},{32,160},{40,168},{48,176},{56,1... | collective-permute-start | bytes 24584 | tf_op jit(solution)/shard_map/ppermute | solution.py:38
  11.9 2.1 %collective-permute-start.10 = (bf16[8,512]{1,0:T(8,128)(2,1)S(1)}, bf16[8,512]{1,0:T(8,128)(2,1)S(1)}, u32[]{:S(2)}, u32[]{:S(2)}) collective-permute-start(bf16[8,512]{1,0:T(8,128)(2,1)S(1)} %slice.133), channel_id=1, source_target_pairs={{0,192},{8,200},{16,208},{24,216},{32,224},{40,232},{48,240},{56,2... | collective-permute-start | bytes 24584 | tf_op jit(solution)/shard_map/ppermute | solution.py:38
  14.9 3.3 %collective-permute-start.5 = (bf16[256,512]{1,0:T(8,128)(2,1)S(1)}, bf16[256,512]{1,0:T(8,128)(2,1)S(1)}, u32[]{:S(2)}, u32[]{:S(2)}) collective-permute-start(bf16[256,512]{1,0:T(8,128)(2,1)S(1)} %pad_maximum_fusion.1), channel_id=1, source_target_pairs={{0,7},{1,0},{2,1},{3,2},{4,3},{5,4},{6,5},{7,6},{8,15},{9,8},{10,9... | collective-permute-start | bytes 786440 | tf_op jit(solution)/shard_map/ppermute | solution.py:27
  18.2 2.0 %collective-permute-done = bf16[128,512]{1,0:T(8,128)(2,1)S(1)} collective-permute-done((bf16[128,512]{1,0:T(8,128)(2,1)S(1)}, bf16[128,512]{1,0:T(8,128)(2,1)S(1)}, u32[]{:S(2)}, u32[]{:S(2)}) %collective-permute-start) | collective-permute-done | bytes 131104 | tf_op jit(solution)/shard_map/ppermute | solution.py:27
  22.7 3.8 %collective-permute-start.6 = (bf16[256,512]{1,0:T(8,128)(2,1)S(1)}, bf16[256,512]{1,0:T(8,128)(2,1)S(1)}, u32[]{:S(2)}, u32[]{:S(2)}) collective-permute-start(bf16[256,512]{1,0:T(8,128)(2,1)S(1)} %add_convert_fusion.3), channel_id=1, source_target_pairs={{0,7},{1,0},{2,1},{3,2},{4,3},{5,4},{6,5},{7,6},{8,15},{9,8},{10,9... | collective-permute-start | bytes 786440 | tf_op jit(solution)/shard_map/ppermute | solution.py:27
  26.5 1.4 %collective-permute-done.1 = bf16[256,512]{1,0:T(8,128)(2,1)S(1)} collective-permute-done((bf16[256,512]{1,0:T(8,128)(2,1)S(1)}, bf16[256,512]{1,0:T(8,128)(2,1)S(1)}, u32[]{:S(2)}, u32[]{:S(2)}) %collective-permute-start.1) | collective-permute-done | bytes 262176 | tf_op jit(solution)/shard_map/ppermute | solution.py:27
  28.2 3.3 %collective-permute-start.12 = (bf16[96,512]{1,0:T(8,128)(2,1)S(1)}, bf16[96,512]{1,0:T(8,128)(2,1)S(1)}, u32[]{:S(2)}, u32[]{:S(2)}) collective-permute-start(bf16[96,512]{1,0:T(8,128)(2,1)S(1)} %slice.164), channel_id=1, source_target_pairs={{0,32},{8,40},{16,48},{24,56},{32,0},{40,8},{48,16},{56,24},{64,96... | collective-permute-start | bytes 294920 | tf_op jit(solution)/shard_map/ppermute | solution.py:38
  31.5 1.1 %collective-permute-start.13 = (bf16[96,512]{1,0:T(8,128)(2,1)S(1)}, bf16[96,512]{1,0:T(8,128)(2,1)S(1)}, u32[]{:S(2)}, u32[]{:S(2)}) collective-permute-start(bf16[96,512]{1,0:T(8,128)(2,1)S(1)} %slice.164), channel_id=1, source_target_pairs={{0,48},{8,56},{16,32},{24,40},{32,16},{40,24},{48,0},{56,8},{64,11... | collective-permute-start | bytes 294920 | tf_op jit(solution)/shard_map/ppermute | solution.py:38
  32.7 3.0 %collective-permute-done.2 = bf16[256,512]{1,0:T(8,128)(2,1)S(1)} collective-permute-done((bf16[256,512]{1,0:T(8,128)(2,1)S(1)}, bf16[256,512]{1,0:T(8,128)(2,1)S(1)}, u32[]{:S(2)}, u32[]{:S(2)}) %collective-permute-start.2) | collective-permute-done | bytes 262176 | tf_op jit(solution)/shard_map/ppermute | solution.py:27
  35.8 1.6 %collective-permute-done.13 = bf16[96,512]{1,0:T(8,128)(2,1)S(1)} collective-permute-done((bf16[96,512]{1,0:T(8,128)(2,1)S(1)}, bf16[96,512]{1,0:T(8,128)(2,1)S(1)}, u32[]{:S(2)}, u32[]{:S(2)}) %collective-permute-start.13) | collective-permute-done | bytes 98336 | tf_op jit(solution)/shard_map/ppermute | solution.py:38
  38.0 3.5 %collective-permute-start.7 = (bf16[256,512]{1,0:T(8,128)(2,1)S(1)}, bf16[256,512]{1,0:T(8,128)(2,1)S(1)}, u32[]{:S(2)}, u32[]{:S(2)}) collective-permute-start(bf16[256,512]{1,0:T(8,128)(2,1)S(1)} %add_convert_fusion.2), channel_id=1, source_target_pairs={{0,7},{1,0},{2,1},{3,2},{4,3},{5,4},{6,5},{7,6},{8,15},{9,8},{10,9... | collective-permute-start | bytes 786440 | tf_op jit(solution)/shard_map/ppermute | solution.py:27
  41.5 6.0 %collective-permute-done.7 = bf16[256,512]{1,0:T(8,128)(2,1)S(1)} collective-permute-done((bf16[256,512]{1,0:T(8,128)(2,1)S(1)}, bf16[256,512]{1,0:T(8,128)(2,1)S(1)}, u32[]{:S(2)}, u32[]{:S(2)}) %collective-permute-start.7) | collective-permute-done | bytes 262176 | tf_op jit(solution)/shard_map/ppermute | solution.py:27
  47.5 3.4 %collective-permute-done.3 = bf16[256,512]{1,0:T(8,128)(2,1)S(1)} collective-permute-done((bf16[256,512]{1,0:T(8,128)(2,1)S(1)}, bf16[256,512]{1,0:T(8,128)(2,1)S(1)}, u32[]{:S(2)}, u32[]{:S(2)}) %collective-permute-start.3) | collective-permute-done | bytes 262176 | tf_op jit(solution)/shard_map/ppermute | solution.py:27
  53.3 1.2 %collective-permute-start.18 = (bf16[32,512]{1,0:T(8,128)(2,1)S(1)}, bf16[32,512]{1,0:T(8,128)(2,1)S(1)}, u32[]{:S(2)}, u32[]{:S(2)}) collective-permute-start(bf16[32,512]{1,0:T(8,128)(2,1)S(1)} %get-tuple-element.41), channel_id=1, source_target_pairs={{0,192},{8,200},{16,208},{24,216},{32,224},{40,232},{48,240},{56,2... | collective-permute-start | bytes 98312 | tf_op jit(solution)/shard_map/ppermute | solution.py:38
  54.5 1.2 %collective-permute-start.17 = (bf16[32,512]{1,0:T(8,128)(2,1)S(1)}, bf16[32,512]{1,0:T(8,128)(2,1)S(1)}, u32[]{:S(2)}, u32[]{:S(2)}) collective-permute-start(bf16[32,512]{1,0:T(8,128)(2,1)S(1)} %get-tuple-element.42), channel_id=1, source_target_pairs={{0,128},{8,136},{16,144},{24,152},{32,160},{40,168},{48,176},{56,1... | collective-permute-start | bytes 98312 | tf_op jit(solution)/shard_map/ppermute | solution.py:38
  55.7 1.7 %collective-permute-start.16 = (bf16[96,512]{1,0:T(8,128)(2,1)S(1)}, bf16[96,512]{1,0:T(8,128)(2,1)S(1)}, u32[]{:S(2)}, u32[]{:S(2)}) collective-permute-start(bf16[96,512]{1,0:T(8,128)(2,1)S(1)} %slice.169), channel_id=1, source_target_pairs={{0,64},{8,72},{16,80},{24,88},{32,96},{40,104},{48,112},{56,120},{... | collective-permute-start | bytes 294920 | tf_op jit(solution)/shard_map/ppermute | solution.py:38
  57.5 1.0 %collective-permute-done.18 = bf16[32,512]{1,0:T(8,128)(2,1)S(1)} collective-permute-done((bf16[32,512]{1,0:T(8,128)(2,1)S(1)}, bf16[32,512]{1,0:T(8,128)(2,1)S(1)}, u32[]{:S(2)}, u32[]{:S(2)}) %collective-permute-start.18) | collective-permute-done | bytes 32800 | tf_op jit(solution)/shard_map/ppermute | solution.py:38
  58.5 1.7 %collective-permute-done.17 = bf16[32,512]{1,0:T(8,128)(2,1)S(1)} collective-permute-done((bf16[32,512]{1,0:T(8,128)(2,1)S(1)}, bf16[32,512]{1,0:T(8,128)(2,1)S(1)}, u32[]{:S(2)}, u32[]{:S(2)}) %collective-permute-start.17) | collective-permute-done | bytes 32800 | tf_op jit(solution)/shard_map/ppermute | solution.py:38
  60.9 2.2 %collective-permute-start.21 = (bf16[56,512]{1,0:T(8,128)(2,1)S(1)}, bf16[56,512]{1,0:T(8,128)(2,1)S(1)}, u32[]{:S(2)}, u32[]{:S(2)}) collective-permute-start(bf16[56,512]{1,0:T(8,128)(2,1)S(1)} %pad_maximum_fusion.5), channel_id=1, source_target_pairs={{0,48},{8,56},{16,32},{24,40},{32,16},{40,24},{48,0},{56,8},{64,11... | collective-permute-start | bytes 172040 | tf_op jit(solution)/shard_map/ppermute | solution.py:38
  63.2 1.8 %collective-permute-start.20 = (bf16[56,512]{1,0:T(8,128)(2,1)S(1)}, bf16[56,512]{1,0:T(8,128)(2,1)S(1)}, u32[]{:S(2)}, u32[]{:S(2)}) collective-permute-start(bf16[56,512]{1,0:T(8,128)(2,1)S(1)} %pad_maximum_fusion.4), channel_id=1, source_target_pairs={{0,32},{8,40},{16,48},{24,56},{32,0},{40,8},{48,16},{56,24},{64,96... | collective-permute-start | bytes 172040 | tf_op jit(solution)/shard_map/ppermute | solution.py:38
  65.0 1.3 %collective-permute-done.19 = bf16[120,512]{1,0:T(8,128)(2,1)S(1)} collective-permute-done((bf16[120,512]{1,0:T(8,128)(2,1)S(1)}, bf16[120,512]{1,0:T(8,128)(2,1)S(1)}, u32[]{:S(2)}, u32[]{:S(2)}) %collective-permute-start.19) | collective-permute-done | bytes 122912 | tf_op jit(solution)/shard_map/ppermute | solution.py:38
  66.8 2.0 %collective-permute-done.20 = bf16[56,512]{1,0:T(8,128)(2,1)S(1)} collective-permute-done((bf16[56,512]{1,0:T(8,128)(2,1)S(1)}, bf16[56,512]{1,0:T(8,128)(2,1)S(1)}, u32[]{:S(2)}, u32[]{:S(2)}) %collective-permute-start.20) | collective-permute-done | bytes 57376 | tf_op jit(solution)/shard_map/ppermute | solution.py:38
  (74 shorter events, 8.6 us)
Async XLA Ops:
  0.7 13.4 %copy-start = (bf16[1024,4096]{1,0:T(8,128)(2,1)S(1)}, bf16[1024,4096]{1,0:T(8,128)(2,1)}, u32[]{:S(2)}) copy-start(bf16[1024,4096]{1,0:T(8,128)(2,1)} %charges.7) | copy-start | bytes 25165828
  4.6 10.2 %collective-permute-start.4 = (bf16[128,512]{1,0:T(8,128)(2,1)S(1)}, bf16[128,512]{1,0:T(8,128)(2,1)S(1)}, u32[]{:S(2)}, u32[]{:S(2)}) collective-permute-start(bf16[128,512]{1,0:T(8,128)(2,1)S(1)} %get-tuple-element.45), channel_id=1, source_target_pairs={{0,7},{1,0},{2,1},{3,2},{4,3},{5,4},{6,5},{7,6},{8,15},{9,8},{10,9... | collective-permute-start | bytes 393224 | tf_op jit(solution)/shard_map/ppermute | solution.py:27
  10.5 17.6 %collective-permute-start.9 = (bf16[8,512]{1,0:T(8,128)(2,1)S(1)}, bf16[8,512]{1,0:T(8,128)(2,1)S(1)}, u32[]{:S(2)}, u32[]{:S(2)}) collective-permute-start(bf16[8,512]{1,0:T(8,128)(2,1)S(1)} %slice.133), channel_id=1, source_target_pairs={{0,128},{8,136},{16,144},{24,152},{32,160},{40,168},{48,176},{56,1... | collective-permute-start | bytes 24584 | tf_op jit(solution)/shard_map/ppermute | solution.py:38
  11.9 16.2 %collective-permute-start.10 = (bf16[8,512]{1,0:T(8,128)(2,1)S(1)}, bf16[8,512]{1,0:T(8,128)(2,1)S(1)}, u32[]{:S(2)}, u32[]{:S(2)}) collective-permute-start(bf16[8,512]{1,0:T(8,128)(2,1)S(1)} %slice.133), channel_id=1, source_target_pairs={{0,192},{8,200},{16,208},{24,216},{32,224},{40,232},{48,240},{56,2... | collective-permute-start | bytes 24584 | tf_op jit(solution)/shard_map/ppermute | solution.py:38
  14.0 6.2 %collective-permute-start = (bf16[128,512]{1,0:T(8,128)(2,1)S(1)}, bf16[128,512]{1,0:T(8,128)(2,1)S(1)}, u32[]{:S(2)}, u32[]{:S(2)}) collective-permute-start(bf16[128,512]{1,0:T(8,128)(2,1)S(1)} %get-tuple-element.44), channel_id=1, source_target_pairs={{0,1},{1,2},{2,3},{3,4},{4,5},{5,6},{6,7},{7,0},{8,9},{9,10},{10,1... | collective-permute-start | bytes 393224 | tf_op jit(solution)/shard_map/ppermute | solution.py:27
  14.0 14.1 %collective-permute-start.8 = (bf16[24,512]{1,0:T(8,128)(2,1)S(1)}, bf16[24,512]{1,0:T(8,128)(2,1)S(1)}, u32[]{:S(2)}, u32[]{:S(2)}) collective-permute-start(bf16[24,512]{1,0:T(8,128)(2,1)S(1)} %slice.132), channel_id=1, source_target_pairs={{0,64},{8,72},{16,80},{24,88},{32,96},{40,104},{48,112},{56,120},{... | collective-permute-start | bytes 73736 | tf_op jit(solution)/shard_map/ppermute | solution.py:38
  14.9 7.7 %collective-permute-start.5 = (bf16[256,512]{1,0:T(8,128)(2,1)S(1)}, bf16[256,512]{1,0:T(8,128)(2,1)S(1)}, u32[]{:S(2)}, u32[]{:S(2)}) collective-permute-start(bf16[256,512]{1,0:T(8,128)(2,1)S(1)} %pad_maximum_fusion.1), channel_id=1, source_target_pairs={{0,7},{1,0},{2,1},{3,2},{4,3},{5,4},{6,5},{7,6},{8,15},{9,8},{10,9... | collective-permute-start | bytes 786440 | tf_op jit(solution)/shard_map/ppermute | solution.py:27
  20.3 7.7 %collective-permute-start.1 = (bf16[256,512]{1,0:T(8,128)(2,1)S(1)}, bf16[256,512]{1,0:T(8,128)(2,1)S(1)}, u32[]{:S(2)}, u32[]{:S(2)}) collective-permute-start(bf16[256,512]{1,0:T(8,128)(2,1)S(1)} %pad_maximum_fusion), channel_id=1, source_target_pairs={{0,1},{1,2},{2,3},{3,4},{4,5},{5,6},{6,7},{7,0},{8,9},{9,10},{10,1... | collective-permute-start | bytes 786440 | tf_op jit(solution)/shard_map/ppermute | solution.py:27
  22.7 9.9 %collective-permute-start.6 = (bf16[256,512]{1,0:T(8,128)(2,1)S(1)}, bf16[256,512]{1,0:T(8,128)(2,1)S(1)}, u32[]{:S(2)}, u32[]{:S(2)}) collective-permute-start(bf16[256,512]{1,0:T(8,128)(2,1)S(1)} %add_convert_fusion.3), channel_id=1, source_target_pairs={{0,7},{1,0},{2,1},{3,2},{4,3},{5,4},{6,5},{7,6},{8,15},{9,8},{10,9... | collective-permute-start | bytes 786440 | tf_op jit(solution)/shard_map/ppermute | solution.py:27
  28.0 7.7 %collective-permute-start.2 = (bf16[256,512]{1,0:T(8,128)(2,1)S(1)}, bf16[256,512]{1,0:T(8,128)(2,1)S(1)}, u32[]{:S(2)}, u32[]{:S(2)}) collective-permute-start(bf16[256,512]{1,0:T(8,128)(2,1)S(1)} %add_convert_fusion.5), channel_id=1, source_target_pairs={{0,1},{1,2},{2,3},{3,4},{4,5},{5,6},{6,7},{7,0},{8,9},{9,10},{10,1... | collective-permute-start | bytes 786440 | tf_op jit(solution)/shard_map/ppermute | solution.py:27
  28.2 7.5 %collective-permute-start.12 = (bf16[96,512]{1,0:T(8,128)(2,1)S(1)}, bf16[96,512]{1,0:T(8,128)(2,1)S(1)}, u32[]{:S(2)}, u32[]{:S(2)}) collective-permute-start(bf16[96,512]{1,0:T(8,128)(2,1)S(1)} %slice.164), channel_id=1, source_target_pairs={{0,32},{8,40},{16,48},{24,56},{32,0},{40,8},{48,16},{56,24},{64,96... | collective-permute-start | bytes 294920 | tf_op jit(solution)/shard_map/ppermute | solution.py:38
  31.5 5.8 %collective-permute-start.13 = (bf16[96,512]{1,0:T(8,128)(2,1)S(1)}, bf16[96,512]{1,0:T(8,128)(2,1)S(1)}, u32[]{:S(2)}, u32[]{:S(2)}) collective-permute-start(bf16[96,512]{1,0:T(8,128)(2,1)S(1)} %slice.164), channel_id=1, source_target_pairs={{0,48},{8,56},{16,32},{24,40},{32,16},{40,24},{48,0},{56,8},{64,11... | collective-permute-start | bytes 294920 | tf_op jit(solution)/shard_map/ppermute | solution.py:38
  32.6 5.3 %collective-permute-start.11 = (bf16[160,512]{1,0:T(8,128)(2,1)S(1)}, bf16[160,512]{1,0:T(8,128)(2,1)S(1)}, u32[]{:S(2)}, u32[]{:S(2)}) collective-permute-start(bf16[160,512]{1,0:T(8,128)(2,1)S(1)} %slice.163), channel_id=1, source_target_pairs={{0,16},{8,24},{16,0},{24,8},{32,48},{40,56},{48,32},{56,40},{64,80... | collective-permute-start | bytes 491528 | tf_op jit(solution)/shard_map/ppermute | solution.py:38
  37.9 13.2 %collective-permute-start.14 = (bf16[640,512]{1,0:T(8,128)(2,1)S(1)}, bf16[640,512]{1,0:T(8,128)(2,1)S(1)}, u32[]{:S(2)}, u32[]{:S(2)}) collective-permute-start(bf16[640,512]{1,0:T(8,128)(2,1)S(1)} %constant_dynamic-update-slice_fusion.5.w), channel_id=1, source_target_pairs={{0,8},{8,0},{16,24},{24,16},{32,40},{40,32},{48,56},{56,48},{64,72... | collective-permute-start | bytes 1966088 | tf_op jit(solution)/shard_map/ppermute | solution.py:38
  38.0 9.4 %collective-permute-start.7 = (bf16[256,512]{1,0:T(8,128)(2,1)S(1)}, bf16[256,512]{1,0:T(8,128)(2,1)S(1)}, u32[]{:S(2)}, u32[]{:S(2)}) collective-permute-start(bf16[256,512]{1,0:T(8,128)(2,1)S(1)} %add_convert_fusion.2), channel_id=1, source_target_pairs={{0,7},{1,0},{2,1},{3,2},{4,3},{5,4},{6,5},{7,6},{8,15},{9,8},{10,9... | collective-permute-start | bytes 786440 | tf_op jit(solution)/shard_map/ppermute | solution.py:27
  41.5 9.4 %collective-permute-start.3 = (bf16[256,512]{1,0:T(8,128)(2,1)S(1)}, bf16[256,512]{1,0:T(8,128)(2,1)S(1)}, u32[]{:S(2)}, u32[]{:S(2)}) collective-permute-start(bf16[256,512]{1,0:T(8,128)(2,1)S(1)} %add_convert_fusion.4), channel_id=1, source_target_pairs={{0,1},{1,2},{2,3},{3,4},{4,5},{5,6},{6,7},{7,0},{8,9},{9,10},{10,1... | collective-permute-start | bytes 786440 | tf_op jit(solution)/shard_map/ppermute | solution.py:27
  51.0 18.6 %copy-start.1 = (bf16[256,512]{1,0:T(8,128)(2,1)}, bf16[256,512]{1,0:T(8,128)(2,1)S(1)}, u32[]{:S(2)}) copy-start(bf16[256,512]{1,0:T(8,128)(2,1)S(1)} %add_convert_fusion.1) | copy-start | bytes 786436
  51.0 1.6 %collective-permute-start.15 = (bf16[256,512]{1,0:T(8,128)(2,1)S(1)}, bf16[256,512]{1,0:T(8,128)(2,1)S(1)}, u32[]{:S(2)}, u32[]{:S(2)}) collective-permute-start(bf16[256,512]{1,0:T(8,128)(2,1)S(1)} %add_convert_fusion.1), channel_id=1, source_target_pairs={{0,8},{8,0},{16,24},{24,16},{32,40},{40,32},{48,56},{56,48},{64,72... | collective-permute-start | bytes 786440 | tf_op jit(solution)/shard_map/ppermute | solution.py:38
  53.3 5.2 %collective-permute-start.18 = (bf16[32,512]{1,0:T(8,128)(2,1)S(1)}, bf16[32,512]{1,0:T(8,128)(2,1)S(1)}, u32[]{:S(2)}, u32[]{:S(2)}) collective-permute-start(bf16[32,512]{1,0:T(8,128)(2,1)S(1)} %get-tuple-element.41), channel_id=1, source_target_pairs={{0,192},{8,200},{16,208},{24,216},{32,224},{40,232},{48,240},{56,2... | collective-permute-start | bytes 98312 | tf_op jit(solution)/shard_map/ppermute | solution.py:38
  54.5 5.7 %collective-permute-start.17 = (bf16[32,512]{1,0:T(8,128)(2,1)S(1)}, bf16[32,512]{1,0:T(8,128)(2,1)S(1)}, u32[]{:S(2)}, u32[]{:S(2)}) collective-permute-start(bf16[32,512]{1,0:T(8,128)(2,1)S(1)} %get-tuple-element.42), channel_id=1, source_target_pairs={{0,128},{8,136},{16,144},{24,152},{32,160},{40,168},{48,176},{56,1... | collective-permute-start | bytes 98312 | tf_op jit(solution)/shard_map/ppermute | solution.py:38
  55.7 5.0 %collective-permute-start.16 = (bf16[96,512]{1,0:T(8,128)(2,1)S(1)}, bf16[96,512]{1,0:T(8,128)(2,1)S(1)}, u32[]{:S(2)}, u32[]{:S(2)}) collective-permute-start(bf16[96,512]{1,0:T(8,128)(2,1)S(1)} %slice.169), channel_id=1, source_target_pairs={{0,64},{8,72},{16,80},{24,88},{32,96},{40,104},{48,112},{56,120},{... | collective-permute-start | bytes 294920 | tf_op jit(solution)/shard_map/ppermute | solution.py:38
  60.8 5.5 %collective-permute-start.19 = (bf16[120,512]{1,0:T(8,128)(2,1)S(1)}, bf16[120,512]{1,0:T(8,128)(2,1)S(1)}, u32[]{:S(2)}, u32[]{:S(2)}) collective-permute-start(bf16[120,512]{1,0:T(8,128)(2,1)S(1)} %pad_maximum_fusion.3), channel_id=1, source_target_pairs={{0,16},{8,24},{16,0},{24,8},{32,48},{40,56},{48,32},{56,40},{64,80... | collective-permute-start | bytes 368648 | tf_op jit(solution)/shard_map/ppermute | solution.py:38
  60.9 5.9 %collective-permute-start.21 = (bf16[56,512]{1,0:T(8,128)(2,1)S(1)}, bf16[56,512]{1,0:T(8,128)(2,1)S(1)}, u32[]{:S(2)}, u32[]{:S(2)}) collective-permute-start(bf16[56,512]{1,0:T(8,128)(2,1)S(1)} %pad_maximum_fusion.5), channel_id=1, source_target_pairs={{0,48},{8,56},{16,32},{24,40},{32,16},{40,24},{48,0},{56,8},{64,11... | collective-permute-start | bytes 172040 | tf_op jit(solution)/shard_map/ppermute | solution.py:38
  63.2 5.7 %collective-permute-start.20 = (bf16[56,512]{1,0:T(8,128)(2,1)S(1)}, bf16[56,512]{1,0:T(8,128)(2,1)S(1)}, u32[]{:S(2)}, u32[]{:S(2)}) collective-permute-start(bf16[56,512]{1,0:T(8,128)(2,1)S(1)} %pad_maximum_fusion.4), channel_id=1, source_target_pairs={{0,32},{8,40},{16,48},{24,56},{32,0},{40,8},{48,16},{56,24},{64,96... | collective-permute-start | bytes 172040 | tf_op jit(solution)/shard_map/ppermute | solution.py:38
  (1 other events, 9.9 us)

commit v2 on v1

--- a/solution.py
+++ b/solution.py
@@ -19,17 +19,14 @@
 
 
 def shift(x, distance):
-    leaves, n = lax.axis_size("leaf"), lax.axis_size("rhs")
-    pairs = []
-    for leaf in range(leaves):
-        step = distance
-        pairs += [(leaf * n + i, leaf * n + (i + step) % n) for i in range(n)]
-    return lax.ppermute(x, ("leaf", "rhs"), pairs)
+    n = lax.axis_size("rhs")
+    pairs = [(i, (i + (-distance if i % 2 else distance)) % n) for i in range(n)]
+    return lax.ppermute(x, "rhs", pairs)
 
 
 def column(place, rel, width):
     n = len(ORDER)
-    block = (place % n + rel) % n
+    block = (place + jnp.where(place % 2 == 0, rel, n - rel)) % n
     return pl.multiple_of(block * width, width)
 
 
@@ -89,10 +86,10 @@
         num_scalar_prefetch=1,
         grid=(1,),
         in_specs=[
-            pl.BlockSpec((1, skel, skel), lambda i, z: (14, 0, z[0] % 8 // 4)),
-            pl.BlockSpec((1, skel, skel), lambda i, z: (12 + z[0] % 8 // 4, 0, z[0] // 2 % 2)),
-            pl.BlockSpec((1, skel, skel), lambda i, z: (8 + z[0] % 8 // 2, 0, z[0] % 2)),
-            pl.BlockSpec((1, skel, 2 * skel), lambda i, z: (z[0] % 8, 0, 0)),
+            pl.BlockSpec((1, skel, skel), lambda i, z: (14, 0, z[0] // 4)),
+            pl.BlockSpec((1, skel, skel), lambda i, z: (12 + z[0] // 4, 0, z[0] // 2 % 2)),
+            pl.BlockSpec((1, skel, skel), lambda i, z: (8 + z[0] // 2, 0, z[0] % 2)),
+            pl.BlockSpec((1, skel, 2 * skel), lambda i, z: (z[0], 0, 0)),
             pl.BlockSpec(leaf_coef.shape, lambda i, z: (0, 0, 0)),
             pl.BlockSpec(leaf_rows.shape, lambda i, z: (0, 0)),
             pl.BlockSpec(memory_space=pl.ANY),
@@ -131,32 +128,32 @@
 
 def ring_sum(s, m):
     half = s[0].shape[0] // 2
-    p = shift(s[4][:half], 1)
-    n = shift(s[4][half:], -1)
+    behind = shift(s[4][:half], 1)
+    ahead = shift(s[4][half:], -1)
     m = paced(m, s[4])
     x1 = swap(m[224:248], 8)
     x2 = swap(m[240:248], 16)
     x3 = swap(m[240:248], 24)
 
-    up = jnp.concatenate([add(s[3][:half], p), s[3][half:]], 0)
-    down = jnp.concatenate([s[5][:half], add(s[5][half:], n)], 0)
-    p = shift(up, 1)
-    n = shift(down, -1)
-    up, down = add(s[2], p), add(s[6], n)
-    p = shift(up, 1)
-    n = shift(down, -1)
-    x1, x2, x3, _, _ = lax.optimization_barrier((x1, x2, x3, up, down))
+    one = jnp.concatenate([s[3][:half], add(s[3][half:], ahead)], 0)
+    two = jnp.concatenate([add(s[5][:half], behind), s[5][half:]], 0)
+    behind = shift(one, 1)
+    ahead = shift(two, -1)
+    one, two = add(s[2], ahead), add(s[6], behind)
+    behind = shift(one, 1)
+    ahead = shift(two, -1)
+    x1, x2, x3, _, _ = lax.optimization_barrier((x1, x2, x3, one, two))
     v = jnp.concatenate([m[0:240], x1[0:16], m[240:248], x1[16:24], x2, x3], 0)
     y2 = swap(v[192:288], 4)
     y1 = swap(v[128:288], 2)
     y3 = swap(v[192:288], 6)
-    up, down = add(s[1], p), add(s[7], n)
-    p = shift(up, 1)
-    n = shift(down, -1)
-    y1, y2, y3, _, _ = lax.optimization_barrier((y1, y2, y3, up, down))
+    one, two = add(s[1], ahead), add(s[7], behind)
+    behind = shift(one, 1)
+    ahead = shift(two, -1)
+    y1, y2, y3, _, _ = lax.optimization_barrier((y1, y2, y3, one, two))
     w = jnp.concatenate([v, y1, y2, y3], 0)
     wp = swap(w, 1)
-    return add3(s[0], p, n), w, wp
+    return add3(s[0], behind, ahead), w, wp
 
 
 def compose_kernel(pos, w, wp, q_ref, p1_ref, pn):
@@ -251,7 +248,7 @@
 
 def local(charges, leaf_coef, leaf_rows, local_interp, top_interp):
     pos = lax.axis_index("leaf").astype(jnp.int32)
-    z = (pos % 2 * lax.axis_size("rhs") + lax.axis_index("rhs").astype(jnp.int32)).reshape(1)
+    z = lax.axis_index("rhs").astype(jnp.int32).reshape(1)
     s = {}
     t, s[4] = first_part(z, charges, leaf_coef, leaf_rows, local_interp)
     for rels in ((3, 5), (2, 6), (1, 7, 0)):

time: 70.6 us -> 71 us (level)
  waiting for transfers between devices: 26.2 us -> 30.6 us
  starting transfers between devices: 33 us -> 29 us
    ppermute x8, starting transfers between devices: 16.6 us -> 12.5 us  [shift(): return lax.ppermute(x, 'rhs', pairs)]
    ppermute x14, waiting for transfers between devices: 9.86 us -> 12.9 us  [swap(): return lax.ppermute(x, 'leaf', [(i, i ^ bits) for i in range(n)])]
    ppermute x8, waiting for transfers between devices: 16.4 us -> 17.8 us  [shift(): return lax.ppermute(x, 'rhs', pairs)]
  transfers between devices with their start and end apart: 22 -> 22, of which waited for: 15 -> 14; matrix products, arithmetic and copies ran while one was open for 1% -> 1% of each run, Pallas kernels for 4% -> 4%
where the time goes in v2:
time: 71 us; the launch traced here: 70.1 us
  waiting for transfers between devices  30.6 us (43%)
  starting transfers between devices  29 us (41%)
  Pallas kernels  6.97 us (10%)
  other arithmetic  1.4 us (2%)
  between operations  1.06 us (1%)
  matrix products  0.73 us (1%)
    ppermute x8, waiting for transfers between devices, shift(): return lax.ppermute(x, 'rhs', pairs)  17.8 us
    ppermute x14, starting transfers between devices, swap(): return lax.ppermute(x, 'leaf', [(i, i ^ bits) for i in range(n)])  16.6 us
    ppermute x14, waiting for transfers between devices, swap(): return lax.ppermute(x, 'leaf', [(i, i ^ bits) for i in range(n)])  12.9 us
    ppermute x8, starting transfers between devices, shift(): return lax.ppermute(x, 'rhs', pairs)  12.5 us
    pallas_call x1, Pallas kernels, first_part(): pl.pallas_call(first_kernel, grid_spec=spec, out_shape=[pltpu.VMEM((skel,...  3.89 us
    pallas_call x3, Pallas kernels, block_parts(): pl.pallas_call(functools.partial(blocks_kernel, rels), in_specs=[pl.Block...  2.45 us
  transfers between devices with their start and end apart: 22, of which 14 were waited for; matrix products, arithmetic and copies ran while one was open for 1% of the time, Pallas kernels for 4%

profile of v2, /device:TPU:6, one launch (start us, length us, event | category | flops | bytes accessed | tf_op | source)
XLA Modules:
  0.0 70.1 jit_solution(9429640275220991980)
XLA Ops:
  0.7 3.9 %first_part.1 = (bf16[256,1024]{1,0:T(8,128)(2,1)S(1)}, bf16[256,512]{1,0:T(8,128)(2,1)S(1)}) custom-call(s32[1]{0:T(128)} %bitcast.z_ref, bf16[15,256,512]{2,1,0:T(8,128)(2,1)} %l1.1, bf16[15,256,512]{2,1,0:T(8,128)(2,1)} %l1.1, bf16[15,256,512]{2,1,0:T(8,128)(2,1)} %l1.1, bf16[15,256,512]{2,1,0:T(8,128)(2,1)} %l1.1, bf16[2,256,512]{2,1,0:T(8,128)(2,1)} %coef.1, ...), custom_call_target="tpu_custom_call" | custom-call | tf_op jit(solution)/shard_map/first_part/pallas_call | solution.py:100
  4.6 2.0 %collective-permute-start.4 = (bf16[128,512]{1,0:T(8,128)(2,1)S(1)}, bf16[128,512]{1,0:T(8,128)(2,1)S(1)}, u32[]{:S(2)}, u32[]{:S(2)}) collective-permute-start(bf16[128,512]{1,0:T(8,128)(2,1)S(1)} %get-tuple-element.45), channel_id=1, source_target_pairs={{0,1},{1,0},{2,3},{3,2},{4,5},{5,4},{6,7},{7,6},{8,9},{9,8},{10,11... | collective-permute-start | bytes 393224 | tf_op jit(solution)/shard_map/ppermute | solution.py:24
  6.6 1.4 %collective-permute-start.9 = (bf16[8,512]{1,0:T(8,128)(2,1)S(1)}, bf16[8,512]{1,0:T(8,128)(2,1)S(1)}, u32[]{:S(2)}, u32[]{:S(2)}) collective-permute-start(bf16[8,512]{1,0:T(8,128)(2,1)S(1)} %slice.133), channel_id=1, source_target_pairs={{0,128},{8,136},{16,144},{24,152},{32,160},{40,168},{48,176},{56,1... | collective-permute-start | bytes 24584 | tf_op jit(solution)/shard_map/ppermute | solution.py:35
  8.0 2.1 %collective-permute-start.10 = (bf16[8,512]{1,0:T(8,128)(2,1)S(1)}, bf16[8,512]{1,0:T(8,128)(2,1)S(1)}, u32[]{:S(2)}, u32[]{:S(2)}) collective-permute-start(bf16[8,512]{1,0:T(8,128)(2,1)S(1)} %slice.133), channel_id=1, source_target_pairs={{0,192},{8,200},{16,208},{24,216},{32,224},{40,232},{48,240},{56,2... | collective-permute-start | bytes 24584 | tf_op jit(solution)/shard_map/ppermute | solution.py:35
  10.1 4.9 %collective-permute-start = (bf16[128,512]{1,0:T(8,128)(2,1)S(1)}, bf16[128,512]{1,0:T(8,128)(2,1)S(1)}, u32[]{:S(2)}, u32[]{:S(2)}) collective-permute-start(bf16[128,512]{1,0:T(8,128)(2,1)S(1)} %get-tuple-element.44), channel_id=1, source_target_pairs={{0,7},{1,2},{2,1},{3,4},{4,3},{5,6},{6,5},{7,0},{8,15},{9,10},{10,... | collective-permute-start | bytes 393224 | tf_op jit(solution)/shard_map/ppermute | solution.py:24
  15.1 0.7 %blocks.5 = (bf16[256,512]{1,0:T(8,128)(2,1)S(1)}, bf16[256,512]{1,0:T(8,128)(2,1)S(1)}) custom-call(s32[1]{0:T(128)} %bitcast.z_ref, bf16[256,1024]{1,0:T(8,128)(2,1)S(1)} %get-tuple-element.20.t, bf16[1024,4096]{1,0:T(8,128)(2,1)S(1)} %copy-done), custom_call_target="tpu_custom_call" | custom-call | tf_op jit(solution)/shard_map/blocks/pallas_call | solution.py:119
  16.0 2.9 %collective-permute-done = bf16[128,512]{1,0:T(8,128)(2,1)S(1)} collective-permute-done((bf16[128,512]{1,0:T(8,128)(2,1)S(1)}, bf16[128,512]{1,0:T(8,128)(2,1)S(1)}, u32[]{:S(2)}, u32[]{:S(2)}) %collective-permute-start) | collective-permute-done | bytes 131104 | tf_op jit(solution)/shard_map/ppermute | solution.py:24
  19.9 1.0 %blocks.3 = (bf16[256,512]{1,0:T(8,128)(2,1)S(1)}, bf16[256,512]{1,0:T(8,128)(2,1)S(1)}, bf16[256,512]{1,0:T(8,128)(2,1)S(1)}) custom-call(s32[1]{0:T(128)} %bitcast.z_ref, bf16[256,1024]{1,0:T(8,128)(2,1)S(1)} %get-tuple-element.20.t, bf16[1024,4096]{1,0:T(8,128)(2,1)S(1)} %copy-done), custom_call_target="tpu_custom_call" | custom-call | tf_op jit(solution)/shard_map/blocks/pallas_call | solution.py:119
  20.9 3.3 %collective-permute-done.5 = bf16[256,512]{1,0:T(8,128)(2,1)S(1)} collective-permute-done((bf16[256,512]{1,0:T(8,128)(2,1)S(1)}, bf16[256,512]{1,0:T(8,128)(2,1)S(1)}, u32[]{:S(2)}, u32[]{:S(2)}) %collective-permute-start.5) | collective-permute-done | bytes 262176 | tf_op jit(solution)/shard_map/ppermute | solution.py:24
  24.3 1.8 %collective-permute-done.1 = bf16[256,512]{1,0:T(8,128)(2,1)S(1)} collective-permute-done((bf16[256,512]{1,0:T(8,128)(2,1)S(1)}, bf16[256,512]{1,0:T(8,128)(2,1)S(1)}, u32[]{:S(2)}, u32[]{:S(2)}) %collective-permute-start.1) | collective-permute-done | bytes 262176 | tf_op jit(solution)/shard_map/ppermute | solution.py:24
  26.2 5.1 %collective-permute-start.2 = (bf16[256,512]{1,0:T(8,128)(2,1)S(1)}, bf16[256,512]{1,0:T(8,128)(2,1)S(1)}, u32[]{:S(2)}, u32[]{:S(2)}) collective-permute-start(bf16[256,512]{1,0:T(8,128)(2,1)S(1)} %add_convert_fusion.5), channel_id=1, source_target_pairs={{0,7},{1,2},{2,1},{3,4},{4,3},{5,6},{6,5},{7,0},{8,15},{9,10},{10,... | collective-permute-start | bytes 786440 | tf_op jit(solution)/shard_map/ppermute | solution.py:24
  31.4 3.3 %collective-permute-start.12 = (bf16[96,512]{1,0:T(8,128)(2,1)S(1)}, bf16[96,512]{1,0:T(8,128)(2,1)S(1)}, u32[]{:S(2)}, u32[]{:S(2)}) collective-permute-start(bf16[96,512]{1,0:T(8,128)(2,1)S(1)} %slice.164), channel_id=1, source_target_pairs={{0,32},{8,40},{16,48},{24,56},{32,0},{40,8},{48,16},{56,24},{64,96... | collective-permute-start | bytes 294920 | tf_op jit(solution)/shard_map/ppermute | solution.py:35
  34.7 1.0 %collective-permute-start.13 = (bf16[96,512]{1,0:T(8,128)(2,1)S(1)}, bf16[96,512]{1,0:T(8,128)(2,1)S(1)}, u32[]{:S(2)}, u32[]{:S(2)}) collective-permute-start(bf16[96,512]{1,0:T(8,128)(2,1)S(1)} %slice.164), channel_id=1, source_target_pairs={{0,48},{8,56},{16,32},{24,40},{32,16},{40,24},{48,0},{56,8},{64,11... | collective-permute-start | bytes 294920 | tf_op jit(solution)/shard_map/ppermute | solution.py:35
  35.9 1.7 %collective-permute-done.12 = bf16[96,512]{1,0:T(8,128)(2,1)S(1)} collective-permute-done((bf16[96,512]{1,0:T(8,128)(2,1)S(1)}, bf16[96,512]{1,0:T(8,128)(2,1)S(1)}, u32[]{:S(2)}, u32[]{:S(2)}) %collective-permute-start.12) | collective-permute-done | bytes 98336 | tf_op jit(solution)/shard_map/ppermute | solution.py:35
  37.6 2.9 %collective-permute-done.13 = bf16[96,512]{1,0:T(8,128)(2,1)S(1)} collective-permute-done((bf16[96,512]{1,0:T(8,128)(2,1)S(1)}, bf16[96,512]{1,0:T(8,128)(2,1)S(1)}, u32[]{:S(2)}, u32[]{:S(2)}) %collective-permute-start.13) | collective-permute-done | bytes 98336 | tf_op jit(solution)/shard_map/ppermute | solution.py:35
  41.4 9.7 %collective-permute-done.7 = bf16[256,512]{1,0:T(8,128)(2,1)S(1)} collective-permute-done((bf16[256,512]{1,0:T(8,128)(2,1)S(1)}, bf16[256,512]{1,0:T(8,128)(2,1)S(1)}, u32[]{:S(2)}, u32[]{:S(2)}) %collective-permute-start.7) | collective-permute-done | bytes 262176 | tf_op jit(solution)/shard_map/ppermute | solution.py:24
  53.7 1.3 %collective-permute-start.18 = (bf16[32,512]{1,0:T(8,128)(2,1)S(1)}, bf16[32,512]{1,0:T(8,128)(2,1)S(1)}, u32[]{:S(2)}, u32[]{:S(2)}) collective-permute-start(bf16[32,512]{1,0:T(8,128)(2,1)S(1)} %get-tuple-element.41), channel_id=1, source_target_pairs={{0,192},{8,200},{16,208},{24,216},{32,224},{40,232},{48,240},{56,2... | collective-permute-start | bytes 98312 | tf_op jit(solution)/shard_map/ppermute | solution.py:35
  55.0 2.9 %collective-permute-start.16 = (bf16[96,512]{1,0:T(8,128)(2,1)S(1)}, bf16[96,512]{1,0:T(8,128)(2,1)S(1)}, u32[]{:S(2)}, u32[]{:S(2)}) collective-permute-start(bf16[96,512]{1,0:T(8,128)(2,1)S(1)} %slice.169), channel_id=1, source_target_pairs={{0,64},{8,72},{16,80},{24,88},{32,96},{40,104},{48,112},{56,120},{... | collective-permute-start | bytes 294920 | tf_op jit(solution)/shard_map/ppermute | solution.py:35
  57.9 1.0 %collective-permute-done.18 = bf16[32,512]{1,0:T(8,128)(2,1)S(1)} collective-permute-done((bf16[32,512]{1,0:T(8,128)(2,1)S(1)}, bf16[32,512]{1,0:T(8,128)(2,1)S(1)}, u32[]{:S(2)}, u32[]{:S(2)}) %collective-permute-start.18) | collective-permute-done | bytes 32800 | tf_op jit(solution)/shard_map/ppermute | solution.py:35
  58.9 1.8 %collective-permute-done.17 = bf16[32,512]{1,0:T(8,128)(2,1)S(1)} collective-permute-done((bf16[32,512]{1,0:T(8,128)(2,1)S(1)}, bf16[32,512]{1,0:T(8,128)(2,1)S(1)}, u32[]{:S(2)}, u32[]{:S(2)}) %collective-permute-start.17) | collective-permute-done | bytes 32800 | tf_op jit(solution)/shard_map/ppermute | solution.py:35
  61.4 2.3 %collective-permute-start.21 = (bf16[56,512]{1,0:T(8,128)(2,1)S(1)}, bf16[56,512]{1,0:T(8,128)(2,1)S(1)}, u32[]{:S(2)}, u32[]{:S(2)}) collective-permute-start(bf16[56,512]{1,0:T(8,128)(2,1)S(1)} %pad_maximum_fusion.5), channel_id=1, source_target_pairs={{0,48},{8,56},{16,32},{24,40},{32,16},{40,24},{48,0},{56,8},{64,11... | collective-permute-start | bytes 172040 | tf_op jit(solution)/shard_map/ppermute | solution.py:35
  63.6 1.8 %collective-permute-start.20 = (bf16[56,512]{1,0:T(8,128)(2,1)S(1)}, bf16[56,512]{1,0:T(8,128)(2,1)S(1)}, u32[]{:S(2)}, u32[]{:S(2)}) collective-permute-start(bf16[56,512]{1,0:T(8,128)(2,1)S(1)} %pad_maximum_fusion.4), channel_id=1, source_target_pairs={{0,32},{8,40},{16,48},{24,56},{32,0},{40,8},{48,16},{56,24},{64,96... | collective-permute-start | bytes 172040 | tf_op jit(solution)/shard_map/ppermute | solution.py:35
  65.4 1.3 %collective-permute-done.19 = bf16[120,512]{1,0:T(8,128)(2,1)S(1)} collective-permute-done((bf16[120,512]{1,0:T(8,128)(2,1)S(1)}, bf16[120,512]{1,0:T(8,128)(2,1)S(1)}, u32[]{:S(2)}, u32[]{:S(2)}) %collective-permute-start.19) | collective-permute-done | bytes 122912 | tf_op jit(solution)/shard_map/ppermute | solution.py:35
  67.2 2.1 %collective-permute-done.20 = bf16[56,512]{1,0:T(8,128)(2,1)S(1)} collective-permute-done((bf16[56,512]{1,0:T(8,128)(2,1)S(1)}, bf16[56,512]{1,0:T(8,128)(2,1)S(1)}, u32[]{:S(2)}, u32[]{:S(2)}) %collective-permute-start.20) | collective-permute-done | bytes 57376 | tf_op jit(solution)/shard_map/ppermute | solution.py:35
  (74 shorter events, 6.8 us)
Async XLA Ops:
  0.6 14.4 %copy-start = (bf16[1024,4096]{1,0:T(8,128)(2,1)S(1)}, bf16[1024,4096]{1,0:T(8,128)(2,1)}, u32[]{:S(2)}) copy-start(bf16[1024,4096]{1,0:T(8,128)(2,1)} %charges.7) | copy-start | bytes 25165828
  4.6 11.2 %collective-permute-start.4 = (bf16[128,512]{1,0:T(8,128)(2,1)S(1)}, bf16[128,512]{1,0:T(8,128)(2,1)S(1)}, u32[]{:S(2)}, u32[]{:S(2)}) collective-permute-start(bf16[128,512]{1,0:T(8,128)(2,1)S(1)} %get-tuple-element.45), channel_id=1, source_target_pairs={{0,1},{1,0},{2,3},{3,2},{4,5},{5,4},{6,7},{7,6},{8,9},{9,8},{10,11... | collective-permute-start | bytes 393224 | tf_op jit(solution)/shard_map/ppermute | solution.py:24
  6.6 24.7 %collective-permute-start.9 = (bf16[8,512]{1,0:T(8,128)(2,1)S(1)}, bf16[8,512]{1,0:T(8,128)(2,1)S(1)}, u32[]{:S(2)}, u32[]{:S(2)}) collective-permute-start(bf16[8,512]{1,0:T(8,128)(2,1)S(1)} %slice.133), channel_id=1, source_target_pairs={{0,128},{8,136},{16,144},{24,152},{32,160},{40,168},{48,176},{56,1... | collective-permute-start | bytes 24584 | tf_op jit(solution)/shard_map/ppermute | solution.py:35
  8.0 23.3 %collective-permute-start.10 = (bf16[8,512]{1,0:T(8,128)(2,1)S(1)}, bf16[8,512]{1,0:T(8,128)(2,1)S(1)}, u32[]{:S(2)}, u32[]{:S(2)}) collective-permute-start(bf16[8,512]{1,0:T(8,128)(2,1)S(1)} %slice.133), channel_id=1, source_target_pairs={{0,192},{8,200},{16,208},{24,216},{32,224},{40,232},{48,240},{56,2... | collective-permute-start | bytes 24584 | tf_op jit(solution)/shard_map/ppermute | solution.py:35
  10.1 8.8 %collective-permute-start = (bf16[128,512]{1,0:T(8,128)(2,1)S(1)}, bf16[128,512]{1,0:T(8,128)(2,1)S(1)}, u32[]{:S(2)}, u32[]{:S(2)}) collective-permute-start(bf16[128,512]{1,0:T(8,128)(2,1)S(1)} %get-tuple-element.44), channel_id=1, source_target_pairs={{0,7},{1,2},{2,1},{3,4},{4,3},{5,6},{6,5},{7,0},{8,15},{9,10},{10,... | collective-permute-start | bytes 393224 | tf_op jit(solution)/shard_map/ppermute | solution.py:24
  15.0 16.2 %collective-permute-start.8 = (bf16[24,512]{1,0:T(8,128)(2,1)S(1)}, bf16[24,512]{1,0:T(8,128)(2,1)S(1)}, u32[]{:S(2)}, u32[]{:S(2)}) collective-permute-start(bf16[24,512]{1,0:T(8,128)(2,1)S(1)} %slice.132), channel_id=1, source_target_pairs={{0,64},{8,72},{16,80},{24,88},{32,96},{40,104},{48,112},{56,120},{... | collective-permute-start | bytes 73736 | tf_op jit(solution)/shard_map/ppermute | solution.py:35
  15.9 8.2 %collective-permute-start.5 = (bf16[256,512]{1,0:T(8,128)(2,1)S(1)}, bf16[256,512]{1,0:T(8,128)(2,1)S(1)}, u32[]{:S(2)}, u32[]{:S(2)}) collective-permute-start(bf16[256,512]{1,0:T(8,128)(2,1)S(1)} %pad_maximum_fusion.1), channel_id=1, source_target_pairs={{0,7},{1,2},{2,1},{3,4},{4,3},{5,6},{6,5},{7,0},{8,15},{9,10},{10,... | collective-permute-start | bytes 786440 | tf_op jit(solution)/shard_map/ppermute | solution.py:24
  19.0 7.2 %collective-permute-start.1 = (bf16[256,512]{1,0:T(8,128)(2,1)S(1)}, bf16[256,512]{1,0:T(8,128)(2,1)S(1)}, u32[]{:S(2)}, u32[]{:S(2)}) collective-permute-start(bf16[256,512]{1,0:T(8,128)(2,1)S(1)} %pad_maximum_fusion), channel_id=1, source_target_pairs={{0,1},{1,0},{2,3},{3,2},{4,5},{5,4},{6,7},{7,6},{8,9},{9,8},{10,11... | collective-permute-start | bytes 786440 | tf_op jit(solution)/shard_map/ppermute | solution.py:24
  24.2 11.5 %collective-permute-start.6 = (bf16[256,512]{1,0:T(8,128)(2,1)S(1)}, bf16[256,512]{1,0:T(8,128)(2,1)S(1)}, u32[]{:S(2)}, u32[]{:S(2)}) collective-permute-start(bf16[256,512]{1,0:T(8,128)(2,1)S(1)} %add_convert_fusion.3), channel_id=1, source_target_pairs={{0,1},{1,0},{2,3},{3,2},{4,5},{5,4},{6,7},{7,6},{8,9},{9,8},{10,11... | collective-permute-start | bytes 786440 | tf_op jit(solution)/shard_map/ppermute | solution.py:24
  26.2 9.6 %collective-permute-start.2 = (bf16[256,512]{1,0:T(8,128)(2,1)S(1)}, bf16[256,512]{1,0:T(8,128)(2,1)S(1)}, u32[]{:S(2)}, u32[]{:S(2)}) collective-permute-start(bf16[256,512]{1,0:T(8,128)(2,1)S(1)} %add_convert_fusion.5), channel_id=1, source_target_pairs={{0,7},{1,2},{2,1},{3,4},{4,3},{5,6},{6,5},{7,0},{8,15},{9,10},{10,... | collective-permute-start | bytes 786440 | tf_op jit(solution)/shard_map/ppermute | solution.py:24
  31.4 6.2 %collective-permute-start.12 = (bf16[96,512]{1,0:T(8,128)(2,1)S(1)}, bf16[96,512]{1,0:T(8,128)(2,1)S(1)}, u32[]{:S(2)}, u32[]{:S(2)}) collective-permute-start(bf16[96,512]{1,0:T(8,128)(2,1)S(1)} %slice.164), channel_id=1, source_target_pairs={{0,32},{8,40},{16,48},{24,56},{32,0},{40,8},{48,16},{56,24},{64,96... | collective-permute-start | bytes 294920 | tf_op jit(solution)/shard_map/ppermute | solution.py:35
  34.7 5.8 %collective-permute-start.13 = (bf16[96,512]{1,0:T(8,128)(2,1)S(1)}, bf16[96,512]{1,0:T(8,128)(2,1)S(1)}, u32[]{:S(2)}, u32[]{:S(2)}) collective-permute-start(bf16[96,512]{1,0:T(8,128)(2,1)S(1)} %slice.164), channel_id=1, source_target_pairs={{0,48},{8,56},{16,32},{24,40},{32,16},{40,24},{48,0},{56,8},{64,11... | collective-permute-start | bytes 294920 | tf_op jit(solution)/shard_map/ppermute | solution.py:35
  35.7 5.3 %collective-permute-start.11 = (bf16[160,512]{1,0:T(8,128)(2,1)S(1)}, bf16[160,512]{1,0:T(8,128)(2,1)S(1)}, u32[]{:S(2)}, u32[]{:S(2)}) collective-permute-start(bf16[160,512]{1,0:T(8,128)(2,1)S(1)} %slice.163), channel_id=1, source_target_pairs={{0,16},{8,24},{16,0},{24,8},{32,48},{40,56},{48,32},{56,40},{64,80... | collective-permute-start | bytes 491528 | tf_op jit(solution)/shard_map/ppermute | solution.py:35
  41.1 10.4 %collective-permute-start.14 = (bf16[640,512]{1,0:T(8,128)(2,1)S(1)}, bf16[640,512]{1,0:T(8,128)(2,1)S(1)}, u32[]{:S(2)}, u32[]{:S(2)}) collective-permute-start(bf16[640,512]{1,0:T(8,128)(2,1)S(1)} %constant_dynamic-update-slice_fusion.5.w), channel_id=1, source_target_pairs={{0,8},{8,0},{16,24},{24,16},{32,40},{40,32},{48,56},{56,48},{64,72... | collective-permute-start | bytes 1966088 | tf_op jit(solution)/shard_map/ppermute | solution.py:35
  41.2 9.9 %collective-permute-start.7 = (bf16[256,512]{1,0:T(8,128)(2,1)S(1)}, bf16[256,512]{1,0:T(8,128)(2,1)S(1)}, u32[]{:S(2)}, u32[]{:S(2)}) collective-permute-start(bf16[256,512]{1,0:T(8,128)(2,1)S(1)} %add_convert_fusion.2), channel_id=1, source_target_pairs={{0,7},{1,2},{2,1},{3,4},{4,3},{5,6},{6,5},{7,0},{8,15},{9,10},{10,... | collective-permute-start | bytes 786440 | tf_op jit(solution)/shard_map/ppermute | solution.py:24
  41.3 9.8 %collective-permute-start.3 = (bf16[256,512]{1,0:T(8,128)(2,1)S(1)}, bf16[256,512]{1,0:T(8,128)(2,1)S(1)}, u32[]{:S(2)}, u32[]{:S(2)}) collective-permute-start(bf16[256,512]{1,0:T(8,128)(2,1)S(1)} %add_convert_fusion.4), channel_id=1, source_target_pairs={{0,1},{1,0},{2,3},{3,2},{4,5},{5,4},{6,7},{7,6},{8,9},{9,8},{10,11... | collective-permute-start | bytes 786440 | tf_op jit(solution)/shard_map/ppermute | solution.py:24
  51.2 18.8 %copy-start.1 = (bf16[256,512]{1,0:T(8,128)(2,1)}, bf16[256,512]{1,0:T(8,128)(2,1)S(1)}, u32[]{:S(2)}) copy-start(bf16[256,512]{1,0:T(8,128)(2,1)S(1)} %add_convert_fusion.1) | copy-start | bytes 786436
  51.2 1.8 %collective-permute-start.15 = (bf16[256,512]{1,0:T(8,128)(2,1)S(1)}, bf16[256,512]{1,0:T(8,128)(2,1)S(1)}, u32[]{:S(2)}, u32[]{:S(2)}) collective-permute-start(bf16[256,512]{1,0:T(8,128)(2,1)S(1)} %add_convert_fusion.1), channel_id=1, source_target_pairs={{0,8},{8,0},{16,24},{24,16},{32,40},{40,32},{48,56},{56,48},{64,72... | collective-permute-start | bytes 786440 | tf_op jit(solution)/shard_map/ppermute | solution.py:35
  53.7 5.2 %collective-permute-start.18 = (bf16[32,512]{1,0:T(8,128)(2,1)S(1)}, bf16[32,512]{1,0:T(8,128)(2,1)S(1)}, u32[]{:S(2)}, u32[]{:S(2)}) collective-permute-start(bf16[32,512]{1,0:T(8,128)(2,1)S(1)} %get-tuple-element.41), channel_id=1, source_target_pairs={{0,192},{8,200},{16,208},{24,216},{32,224},{40,232},{48,240},{56,2... | collective-permute-start | bytes 98312 | tf_op jit(solution)/shard_map/ppermute | solution.py:35
  55.0 5.7 %collective-permute-start.17 = (bf16[32,512]{1,0:T(8,128)(2,1)S(1)}, bf16[32,512]{1,0:T(8,128)(2,1)S(1)}, u32[]{:S(2)}, u32[]{:S(2)}) collective-permute-start(bf16[32,512]{1,0:T(8,128)(2,1)S(1)} %get-tuple-element.42), channel_id=1, source_target_pairs={{0,128},{8,136},{16,144},{24,152},{32,160},{40,168},{48,176},{56,1... | collective-permute-start | bytes 98312 | tf_op jit(solution)/shard_map/ppermute | solution.py:35
  55.0 6.2 %collective-permute-start.16 = (bf16[96,512]{1,0:T(8,128)(2,1)S(1)}, bf16[96,512]{1,0:T(8,128)(2,1)S(1)}, u32[]{:S(2)}, u32[]{:S(2)}) collective-permute-start(bf16[96,512]{1,0:T(8,128)(2,1)S(1)} %slice.169), channel_id=1, source_target_pairs={{0,64},{8,72},{16,80},{24,88},{32,96},{40,104},{48,112},{56,120},{... | collective-permute-start | bytes 294920 | tf_op jit(solution)/shard_map/ppermute | solution.py:35
  61.2 5.5 %collective-permute-start.19 = (bf16[120,512]{1,0:T(8,128)(2,1)S(1)}, bf16[120,512]{1,0:T(8,128)(2,1)S(1)}, u32[]{:S(2)}, u32[]{:S(2)}) collective-permute-start(bf16[120,512]{1,0:T(8,128)(2,1)S(1)} %pad_maximum_fusion.3), channel_id=1, source_target_pairs={{0,16},{8,24},{16,0},{24,8},{32,48},{40,56},{48,32},{56,40},{64,80... | collective-permute-start | bytes 368648 | tf_op jit(solution)/shard_map/ppermute | solution.py:35
  61.4 5.9 %collective-permute-start.21 = (bf16[56,512]{1,0:T(8,128)(2,1)S(1)}, bf16[56,512]{1,0:T(8,128)(2,1)S(1)}, u32[]{:S(2)}, u32[]{:S(2)}) collective-permute-start(bf16[56,512]{1,0:T(8,128)(2,1)S(1)} %pad_maximum_fusion.5), channel_id=1, source_target_pairs={{0,48},{8,56},{16,32},{24,40},{32,16},{40,24},{48,0},{56,8},{64,11... | collective-permute-start | bytes 172040 | tf_op jit(solution)/shard_map/ppermute | solution.py:35
  63.6 5.7 %collective-permute-start.20 = (bf16[56,512]{1,0:T(8,128)(2,1)S(1)}, bf16[56,512]{1,0:T(8,128)(2,1)S(1)}, u32[]{:S(2)}, u32[]{:S(2)}) collective-permute-start(bf16[56,512]{1,0:T(8,128)(2,1)S(1)} %pad_maximum_fusion.4), channel_id=1, source_target_pairs={{0,32},{8,40},{16,48},{24,56},{32,0},{40,8},{48,16},{56,24},{64,96... | collective-permute-start | bytes 172040 | tf_op jit(solution)/shard_map/ppermute | solution.py:35
  (1 other events, 6.0 us)
